TPU v7x, 32 devices: a whole 2x2x4 slice. The times are simulated.
32 devices in a mesh: row: 8 (over y, x, core), col: 4 (over z).
Axes of the slice: x: 2, y: 2, z: 4, core: 2. Of those that a mesh axis runs over, the one named last changes fastest.
Arguments:
- features: bfloat16 [4096, 512], P(('row', 'col')), may hold values from -6 to 6
- weight: bfloat16 [512, 512], replicated, may hold values from -0.25 to 0.25
- cotangent: bfloat16 [4096, 512], P(('row', 'col')), may hold values from -6 to 6
- tile_blocks: bfloat16 [64, 128, 128], P(('row', 'col')), may hold values from -0.25 to 0.25
- tile_index: int32 [32, 2], P(('row', 'col')), may hold values from 0 to 3, as said below
- tile_count: int32 [32], P(('row', 'col')), may hold values from 1 to 2, as said below
Outputs:
- out_features: bfloat16 [4096, 512], P(('row', 'col'))
- grad_features: bfloat16 [4096, 512], P(('row', 'col'))
- grad_weight: float32 [512, 512], P('col')
Inputs may be any that keep to these rules, and one draw needn't show every extreme that they name: `tile_index`: in each block's row the first tile_count entries are strictly increasing, and all 2 entries are distinct; slots at or past tile_count are ignored. `tile_count`: some block has exactly 2 live slots.
All inputs are finite; a program needn't handle non-finite values.
Results may differ from a plain program's by a relative error of at most 0.007.
Values may be sent and summed in bfloat16 or wider, within the bound.
No kernel may reach another device: no remote copies, remote signals or barrier semaphores. Data moves between devices by JAX's collectives and lax.ppermute only.
A program may use at most 64 MiB of HBM per device.

v0:
```python
import math

import jax
import jax.numpy as jnp
from jax import lax
from jax.sharding import PartitionSpec as P


def tile_range(tile_col, live_mask, first, extent):
    lower = jnp.sum(jnp.where(live_mask & (tile_col < first), 1, 0)).astype(jnp.int32)
    upper = jnp.sum(jnp.where(live_mask & (tile_col < first + extent), 1, 0)).astype(jnp.int32)
    return (lower, upper)


def on_device(features, weight, cotangent, tile_blocks, tile_index, tile_count):
    rows, width = features.shape
    tile = tile_blocks.shape[1]
    row_tiles = rows // tile
    slots = tile_blocks.shape[0]
    index = tile_index[0]
    live_mask = jnp.arange(slots, dtype=jnp.int32) < tile_count[0]
    tile_col = index // row_tiles
    tile_row = index % row_tiles
    panels = features.reshape(row_tiles, tile, width)
    piece = lax.all_gather(panels, "col", axis=0, tiled=True)
    lower, upper = tile_range(tile_col, live_mask, jnp.int32(0), piece.shape[0])

    def add_step(slot, acc):
        block = lax.dynamic_index_in_dim(tile_blocks, slot, 0, keepdims=False)
        source = lax.dynamic_index_in_dim(piece, tile_col[slot], 0, keepdims=False)
        product = jnp.dot(block, source, preferred_element_type=jnp.float32)
        current = lax.dynamic_index_in_dim(acc, tile_row[slot], 0, keepdims=False)
        return lax.dynamic_update_index_in_dim(acc, current + product, tile_row[slot], 0)

    summed = lax.fori_loop(lower, upper, add_step, panels.astype(jnp.float32))
    aggregated = summed.reshape(rows, width).astype(jnp.bfloat16)
    pre_act = jnp.dot(aggregated, weight, preferred_element_type=jnp.float32)
    sigmoid_pre = jax.nn.sigmoid(pre_act)
    out_features = (pre_act * sigmoid_pre).astype(jnp.bfloat16)
    grad_pre = (
        cotangent.astype(jnp.float32) * sigmoid_pre * (1.0 + pre_act * (1.0 - sigmoid_pre))
    ).astype(jnp.bfloat16)
    node_total = rows * lax.axis_size("row") * lax.axis_size("col")
    local_weight = lax.dot_general(
        aggregated, grad_pre, (((0,), (0,)), ((), ())), preferred_element_type=jnp.float32
    ) * (1.0 / math.sqrt(node_total))
    grad_mid = lax.dot_general(
        grad_pre, weight, (((1,), (1,)), ((), ())), preferred_element_type=jnp.float32
    ).astype(jnp.bfloat16)
    mid_tiles = grad_mid.reshape(row_tiles, tile, width)
    extent = lax.axis_size("col") * rows
    first = jnp.int32(0) // tile
    tiles_here = extent // tile
    lower, upper = tile_range(tile_col, live_mask, first, tiles_here)

    def spread_step(slot, acc):
        block = lax.dynamic_index_in_dim(tile_blocks, slot, 0, keepdims=False)
        source = lax.dynamic_index_in_dim(mid_tiles, tile_row[slot], 0, keepdims=False)
        product = lax.dot_general(
            block, source, (((0,), (0,)), ((), ())), preferred_element_type=jnp.float32
        )
        target = tile_col[slot]
        current = lax.dynamic_index_in_dim(acc, target, 0, keepdims=False)
        return lax.dynamic_update_index_in_dim(acc, current + product, target, 0)

    terms = lax.fori_loop(
        lower, upper, spread_step, jnp.zeros((tiles_here, tile, width), jnp.float32)
    )
    gathered_back = lax.psum_scatter(
        terms.reshape(extent, width).astype(jnp.bfloat16), "col", scatter_dimension=0, tiled=True
    ).astype(jnp.float32)
    grad_features = (grad_mid.astype(jnp.float32) + gathered_back).astype(jnp.bfloat16)
    share = width // lax.axis_size("col")
    total_weight = lax.psum(local_weight, ("row", "col"))
    grad_weight = lax.dynamic_slice_in_dim(total_weight, lax.axis_index("col") * share, share, 0)
    return (out_features, grad_features, grad_weight)


def solution(mesh):
    return jax.shard_map(
        on_device,
        mesh=mesh,
        in_specs=(
            P(("row", "col"), None),
            P(),
            P(("row", "col"), None),
            P(("row", "col"), None, None),
            P(("row", "col"), None),
            P(("row", "col")),
        ),
        out_specs=(P(("row", "col"), None), P(("row", "col"), None), P("col", None)),
        check_vma=False,
    )
```

profile of v0, /device:TPU:0, one launch (start us, length us, event | category | flops | bytes accessed | tf_op | source)
XLA Modules:
  0.0 181.4 jit_solution(5367560793325925598)
XLA Ops:
  8.0 0.0 copy-start
  8.0 0.0 all-reduce.2.cloned.1.call-start
  8.1 1.0 bitcast_convert_fusion
  9.1 0.0 copy-start.1
  9.1 17.5 %all-gather = bf16[512,512]{1,0:T(8,128)(2,1)S(1)} all-gather(bf16[128,512]{1,0:T(8,128)(2,1)S(1)} %copy-done.2), channel_id=2, replica_groups=mesh['row'=8,'col'=4] {'col'}, dimensions={0}, use_global_device_ids=true | all-gather | bytes 655360 | tf_op jit(solution)/shard_map/all_gather | solution.py:25
  27.2 0.6 copy-done.3
  27.9 0.7 fusion.18
  29.2 4.0 %while.22 = (s32[]{:T(128)}, f32[1,128,512]{2,1,0:T(8,128)S(1)}, s32[]{:T(128)}, bf16[2,128,128]{2,1,0:T(8,128)(2,1)S(1)}, s32[2]{0:T(128)S(1)}, /*index=5*/bf16...) while((s32[]{:T(128)}, f32[1,128,512]{2,1,0:T(8,128)S(1)}, s32[]{:T(128)}, ...), condition=%wide.region_3.4_spmd, body=%wide.region_2.3_spmd.sunk | while | flops 16842760 | bytes 688325 | solution.py:35
  29.9 0.6 dynamic_slice.60
  32.4 0.2 fusion.29
  33.2 0.9 multiply_convert_fusion.1
  34.2 1.4 convolution_multiply_fusion
  35.6 0.0 all-reduce.2.cloned.1.call-update
  35.6 0.0 reduce-scatter.2.cloned.1.call-start
  35.7 0.3 convolution_convert_fusion
  36.0 0.1 broadcast_in_dim.23
  36.1 6.5 %while.23 = (s32[]{:T(128)}, f32[4,128,512]{2,1,0:T(8,128)S(1)}, s32[]{:T(128)}, s32[2]{0:T(128)S(1)}, bf16[2,128,128]{2,1,0:T(8,128)(2,1)S(1)}, /*index=5*/bf16...) while((s32[]{:T(128)}, f32[4,128,512]{2,1,0:T(8,128)S(1)}, s32[]{:T(128)}, ...), condition=%wide.region_5.6_spmd, body=%wide.region_4.5_spmd.sunk | while | flops 16842760 | bytes 1212617 | solution.py:66
  38.0 0.6 dynamic_slice.63
  40.6 0.2 fusion.32
  42.6 0.9 convert_element_type.48
  43.5 0.0 reduce-scatter.2.cloned.1.call-update
  43.5 127.2 %all-reduce.2.cloned.1.call-done = f32[512,512]{1,0:T(8,128)} async-done(((f32[512,512]{1,0:T(8,128)}), f32[512,512]{1,0:T(8,128)}) %all-reduce.2.cloned.1.call-update) | async-done | bytes 1048592 | tf_op jit(solution)/shard_map/psum | solution.py:74
  170.7 1.7 constant_dynamic-slice_fusion.1
  172.4 1.6 add_convert_fusion
  (9 shorter events, 0.0 us)
Async XLA Ops:
  8.0 25.2 %copy-start = (bf16[512,512]{1,0:T(8,128)(2,1)S(1)}, bf16[512,512]{1,0:T(8,128)(2,1)}, u32[]{:S(2)}) copy-start(bf16[512,512]{1,0:T(8,128)(2,1)} %param.11) | copy-start | bytes 1572868
  8.0 1.1 copy-start.2
  8.0 162.7 %all-reduce.2.cloned.1.call-start = ((), (), s32[]{:S(2)}) async-start(), calls=%async_computation.2 | async-start | bytes 2097152 | tf_op jit(solution)/shard_map/psum | solution.py:74
  9.1 20.2 %copy-start.1 = (bf16[2,128,128]{2,1,0:T(8,128)(2,1)S(1)}, bf16[2,128,128]{2,1,0:T(8,128)(2,1)}, u32[]{:S(2)}) copy-start(bf16[2,128,128]{2,1,0:T(8,128)(2,1)} %param.13) | copy-start | bytes 196612
  27.2 0.7 copy-start.3
  33.2 0.9 copy-start.4
  35.6 136.8 %reduce-scatter.2.cloned.1.call-start = ((), (), s32[]{:S(2)}) async-start(), calls=%async_computation.1 | async-start | bytes 655360 | tf_op jit(solution)/shard_map/reduce_scatter | solution.py:69
Sparse Core Ops, SparseCore 0:
  35.7 134.9 all-reduce.1
Sparse Core Ops, SparseCore 1:
  43.6 29.1 reduce-scatter.1
where the time goes:
time: 183 us; the launch traced here: 181 us
  waiting for transfers between devices  127 us (69%)
  blocking collectives  17.5 us (10%)
  between operations  16.9 us (9%)
  loops' own time  8.88 us (5%)
  other arithmetic  4.13 us (2%)
  local copies, waits for them, and re-layouts  3.66 us (2%)
  matrix products  3.04 us (2%)
    psum x1, waiting for transfers between devices, on_device(): total_weight = lax.psum(local_weight, ('row', 'col'))  127 us
    all_gather x1, blocking collectives, on_device(): piece = lax.all_gather(panels, 'col', axis=0, tiled=True)  17.5 us
    another operation x1, loops' own time, on_device(): lax.fori_loop(lower, upper, spread_step, jnp.zeros((tiles_here, tile, wid...  5.67 us
  transfers between devices with their start and end apart: 2, of which 1 were waited for; matrix products, arithmetic and copies ran while one was open for 2% of the time, Pallas kernels for 0%

commit v1 on v0

v1 whole, which is shorter than its diff:
```python
import functools
import math

import jax
import jax.numpy as jnp
from jax import lax
from jax.experimental import pallas as pl
from jax.experimental.pallas import tpu as pltpu
from jax.sharding import PartitionSpec as P

F32 = jnp.float32
BF16 = jnp.bfloat16


def tile_range(tile_col, live_mask, first, extent):
    lower = jnp.sum(jnp.where(live_mask & (tile_col < first), 1, 0)).astype(jnp.int32)
    upper = jnp.sum(jnp.where(live_mask & (tile_col < first + extent), 1, 0)).astype(jnp.int32)
    return (lower, upper)


def any_mesh(features, weight, cotangent, tile_blocks, tile_index, tile_count):
    rows, width = features.shape
    tile = tile_blocks.shape[1]
    row_tiles = rows // tile
    slots = tile_blocks.shape[0]
    index = tile_index[0]
    live_mask = jnp.arange(slots, dtype=jnp.int32) < tile_count[0]
    tile_col = index // row_tiles
    tile_row = index % row_tiles
    panels = features.reshape(row_tiles, tile, width)
    piece = lax.all_gather(panels, "col", axis=0, tiled=True)
    lower, upper = tile_range(tile_col, live_mask, jnp.int32(0), piece.shape[0])

    def add_step(slot, acc):
        block = lax.dynamic_index_in_dim(tile_blocks, slot, 0, keepdims=False)
        source = lax.dynamic_index_in_dim(piece, tile_col[slot], 0, keepdims=False)
        product = jnp.dot(block, source, preferred_element_type=F32)
        current = lax.dynamic_index_in_dim(acc, tile_row[slot], 0, keepdims=False)
        return lax.dynamic_update_index_in_dim(acc, current + product, tile_row[slot], 0)

    summed = lax.fori_loop(lower, upper, add_step, panels.astype(F32))
    aggregated = summed.reshape(rows, width).astype(BF16)
    pre_act = jnp.dot(aggregated, weight, preferred_element_type=F32)
    sigmoid_pre = jax.nn.sigmoid(pre_act)
    out_features = (pre_act * sigmoid_pre).astype(BF16)
    grad_pre = (
        cotangent.astype(F32) * sigmoid_pre * (1.0 + pre_act * (1.0 - sigmoid_pre))
    ).astype(BF16)
    node_total = rows * lax.axis_size("row") * lax.axis_size("col")
    local_weight = lax.dot_general(
        aggregated, grad_pre, (((0,), (0,)), ((), ())), preferred_element_type=F32
    ) * (1.0 / math.sqrt(node_total))
    grad_mid = lax.dot_general(
        grad_pre, weight, (((1,), (1,)), ((), ())), preferred_element_type=F32
    ).astype(BF16)
    mid_tiles = grad_mid.reshape(row_tiles, tile, width)
    extent = lax.axis_size("col") * rows
    first = jnp.int32(0) // tile
    tiles_here = extent // tile
    lower, upper = tile_range(tile_col, live_mask, first, tiles_here)

    def spread_step(slot, acc):
        block = lax.dynamic_index_in_dim(tile_blocks, slot, 0, keepdims=False)
        source = lax.dynamic_index_in_dim(mid_tiles, tile_row[slot], 0, keepdims=False)
        product = lax.dot_general(
            block, source, (((0,), (0,)), ((), ())), preferred_element_type=F32
        )
        target = tile_col[slot]
        current = lax.dynamic_index_in_dim(acc, target, 0, keepdims=False)
        return lax.dynamic_update_index_in_dim(acc, current + product, target, 0)

    terms = lax.fori_loop(
        lower, upper, spread_step, jnp.zeros((tiles_here, tile, width), F32)
    )
    gathered_back = lax.psum_scatter(
        terms.reshape(extent, width).astype(BF16), "col", scatter_dimension=0, tiled=True
    ).astype(F32)
    grad_features = (grad_mid.astype(F32) + gathered_back).astype(BF16)
    share = width // lax.axis_size("col")
    total_weight = lax.psum(local_weight, ("row", "col"))
    grad_weight = lax.dynamic_slice_in_dim(total_weight, lax.axis_index("col") * share, share, 0)
    return (out_features, grad_features, grad_weight)


def swap(value, axis, mask, size):
    return lax.ppermute(value, axis, [(i, i ^ mask) for i in range(size)])


def vmem(count):
    return [pl.BlockSpec(memory_space=pltpu.VMEM)] * count


def forward_kernel(scale, slots, where, f0, f1, f2, f3, tp0, tp1, ct0, ct1, w,
                   out, gp, sel, keep, send, adj, agg, gw):
    tile = f0.shape[0]
    own, half = where[0], where[1]
    for b, tp in enumerate((tp0, tp1)):
        for t in range(4):
            name = (own ^ t).astype(F32)
            total = jnp.zeros((tile, tile), BF16)
            for s in range(slots):
                mark = tp[pl.ds(slots * tile + 16 * s, 16), :][0:1, :].astype(F32)
                block = tp[pl.ds(s * tile, tile), :]
                total = total + jnp.where(mark == name, block.astype(F32), 0.0).astype(BF16)
            adj[pl.ds(b * tile, tile), pl.ds(t * tile, tile)] = total
    near = jnp.concatenate([f0[...], f1[...]], axis=0)
    far = jnp.concatenate([f2[...], f3[...]], axis=0)
    summed = near.astype(F32)
    summed = summed + jnp.dot(adj[:, : 2 * tile], near, preferred_element_type=F32)
    summed = summed + jnp.dot(adj[:, 2 * tile :], far, preferred_element_type=F32)
    agg[...] = summed.astype(BF16)
    pre = jnp.dot(agg[...], w[...], preferred_element_type=F32)
    sig = jax.nn.sigmoid(pre)
    out[...] = (pre[:tile] * sig[:tile]).astype(BF16)
    cot = jnp.concatenate([ct0[...], ct1[...]], axis=0).astype(F32)
    gp[...] = (cot * sig * (1.0 + pre * (1.0 - sig))).astype(BF16)
    sel[:, :tile] = adj[:, :tile]
    sel[:, tile:] = adj[:, 2 * tile : 3 * tile]
    for b in range(2):
        lane = pl.multiple_of((own ^ (2 * b)) * tile, tile)
        gw[pl.ds(b * tile, tile), :] = lax.dot_general(
            agg[:, pl.ds(lane, tile)], gp[...], (((0,), (0,)), ((), ())),
            preferred_element_type=F32,
        ) * scale
        part = tile // 2
        mine = pl.multiple_of(b * tile + half * part, part)
        other = pl.multiple_of(b * tile + (1 - half) * part, part)
        keep[b] = gw[pl.ds(mine, part), :]
        send[b] = gw[pl.ds(other, part), :].astype(BF16)


def backward_kernel(gp, sel, w, back, part):
    tile = gp.shape[0] // 2
    mid = lax.dot_general(
        gp[...], w[...], (((1,), (1,)), ((), ())), preferred_element_type=F32
    ).astype(BF16)
    terms = lax.dot_general(
        sel[...], mid, (((0,), (0,)), ((), ())), preferred_element_type=F32
    )
    back[...] = terms[tile:].astype(BF16)
    part[...] = mid[:tile].astype(F32) + terms[:tile]


def four_by_eight(features, weight, cotangent, tile_blocks, tile_index, tile_count):
    rows, width = features.shape
    slots, tile, _ = tile_blocks.shape
    own = lax.axis_index("col")
    half = lax.axis_index("row") & 1
    f3 = swap(features, "col", 3, 4)
    f2 = swap(features, "col", 2, 4)
    f1 = swap(features, "col", 1, 4)
    ct1 = swap(cotangent, "col", 1, 4)
    live = jnp.arange(slots, dtype=jnp.int32) < tile_count[0]
    marks = jnp.where(live, tile_index[0], -1).astype(BF16)
    marks = jnp.broadcast_to(marks[:, None, None], (slots, 16, tile)).reshape(slots * 16, tile)
    tp0 = jnp.concatenate([tile_blocks.reshape(slots * tile, tile), marks], axis=0)
    tp1 = swap(tp0, "col", 1, 4)
    where = jnp.stack([own, half]).astype(jnp.int32)
    scale = 1.0 / math.sqrt(rows * lax.axis_size("row") * lax.axis_size("col"))
    out, gp, sel, keep, send = pl.pallas_call(
        functools.partial(forward_kernel, scale, slots),
        out_shape=(
            jax.ShapeDtypeStruct((rows, width), BF16),
            jax.ShapeDtypeStruct((2 * rows, width), BF16),
            jax.ShapeDtypeStruct((2 * rows, 2 * tile), BF16),
            jax.ShapeDtypeStruct((2, tile // 2, width), F32),
            jax.ShapeDtypeStruct((2, tile // 2, width), BF16),
        ),
        in_specs=[pl.BlockSpec(memory_space=pltpu.SMEM)] + vmem(9),
        out_specs=tuple(vmem(5)),
        scratch_shapes=[
            pltpu.VMEM((2 * tile, 4 * tile), BF16),
            pltpu.VMEM((2 * tile, width), BF16),
            pltpu.VMEM((2 * tile, width), F32),
        ],
        cost_estimate=pl.CostEstimate(
            flops=2 * 256 * 512 * 512 * 3, bytes_accessed=3 << 20, transcendentals=256 * 512
        ),
    )(where, features, f1, f2, f3, tp0, tp1, cotangent, ct1, weight)
    got = swap(send, "row", 1, 8)
    summed = keep + got.astype(F32)
    got = swap(summed[1].astype(BF16), "col", 2, 4)
    mine = (summed[0] + got.astype(F32)).astype(BF16)
    back, part = pl.pallas_call(
        backward_kernel,
        out_shape=(
            jax.ShapeDtypeStruct((rows, width), BF16),
            jax.ShapeDtypeStruct((rows, width), F32),
        ),
        in_specs=vmem(3),
        out_specs=tuple(vmem(2)),
        cost_estimate=pl.CostEstimate(
            flops=2 * 256 * 512 * 512 * 2, bytes_accessed=2 << 20, transcendentals=0
        ),
    )(gp, sel, weight)
    got_back = swap(back, "col", 2, 4)
    diagonal = swap(mine, "row", 6, 8).astype(F32)
    along = swap(mine, "row", 4, 8).astype(F32)
    across = swap(mine, "row", 2, 8).astype(F32)
    total = (mine.astype(F32) + across) + (along + diagonal)
    rest = swap(total, "row", 1, 8)
    first = jnp.where(half == 0, total, rest)
    second = jnp.where(half == 0, rest, total)
    grad_weight = jnp.concatenate([first, second], axis=0)
    grad_features = (part + got_back.astype(F32)).astype(BF16)
    return (out, grad_features, grad_weight)


def solution(mesh):
    sizes = (mesh.shape["row"], mesh.shape["col"])

    def on_device(*args):
        rows, width = args[0].shape
        tile = args[3].shape[1]
        small = sizes == (8, 4) and rows == tile and width == 4 * tile
        return (four_by_eight if small else any_mesh)(*args)

    return jax.shard_map(
        on_device,
        mesh=mesh,
        in_specs=(
            P(("row", "col"), None),
            P(),
            P(("row", "col"), None),
            P(("row", "col"), None, None),
            P(("row", "col"), None),
            P(("row", "col")),
        ),
        out_specs=(P(("row", "col"), None), P(("row", "col"), None), P("col", None)),
        check_vma=False,
    )
```

time: 183 us -> 47.1 us (0.26)
  waiting for transfers between devices: 127 us -> 20.9 us
  blocking collectives: 17.5 us -> 0 us
  between operations: 16.9 us -> 1.4 us
  starting transfers between devices: 0.08 us -> 12.8 us
  loops' own time: 8.88 us -> 0 us
  Pallas kernels: 0 us -> 5.51 us
  matrix products: 3.04 us -> 0 us
    psum x1 -> x0, waiting for transfers between devices: 127 us -> none  [on_device(): total_weight = lax.psum(local_weight, ('row', 'col'))]
    ppermute x0 -> x12, waiting for transfers between devices: none -> 20.9 us  [swap(): return lax.ppermute(value, axis, [(i, i ^ mask) for i in range(size)])]
    all_gather x1 -> x0, blocking collectives: 17.5 us -> none  [on_device(): piece = lax.all_gather(panels, 'col', axis=0, tiled=True)]
    ppermute x0 -> x12, starting transfers between devices: none -> 12.8 us  [swap(): return lax.ppermute(value, axis, [(i, i ^ mask) for i in range(size)])]
    another operation x2 -> x0, loops' own time: 8.88 us -> none  [the longest x1 5.67 us: on_device(): lax.fori_loop(lower, upper, spread_step, jnp.zeros((tiles_here, tile, wid...]
    pallas_call x0 -> x2, Pallas kernels: none -> 5.51 us  [the longest x1 3.08 us: four_by_eight(): pl.pallas_call(functools.partial(forward_kernel, scale, slots), out_shape...]
    dot_general x5 -> x0, matrix products: 3.04 us -> none  [the longest x1 1.39 us: on_device(): lax.dot_general(aggregated, grad_pre, (((0,), (0,)), ((), ())), preferred...]
    dynamic_slice x4 -> x0, local copies, waits for them, and re-layouts: 2.87 us -> none  [the longest x1 1.67 us: on_device(): lax.dynamic_slice_in_dim(total_weight, lax.axis_index('col') * share, sha...]
  transfers between devices with their start and end apart: 2 -> 12, of which waited for: 1 -> 6; matrix products, arithmetic and copies ran while one was open for 2% -> 5% of each run, Pallas kernels for 0% -> 5%
where the time goes in v1:
time: 47.1 us; the launch traced here: 46.8 us
  waiting for transfers between devices  20.9 us (44%)
  starting transfers between devices  12.8 us (27%)
  Pallas kernels  5.51 us (12%)
  other arithmetic  4 us (8%)
  local copies, waits for them, and re-layouts  2.2 us (5%)
  between operations  1.4 us (3%)
    ppermute x12, waiting for transfers between devices, swap(): return lax.ppermute(value, axis, [(i, i ^ mask) for i in range(size)])  20.9 us
    ppermute x12, starting transfers between devices, swap(): return lax.ppermute(value, axis, [(i, i ^ mask) for i in range(size)])  12.8 us
    pallas_call x1, Pallas kernels, four_by_eight(): pl.pallas_call(functools.partial(forward_kernel, scale, slots), out_shape...  3.08 us
    pallas_call x1, Pallas kernels, four_by_eight(): pl.pallas_call(backward_kernel, out_shape=(jax.ShapeDtypeStruct((rows, wi...  2.43 us
    unnamed x16, local copies, waits for them, and re-layouts  2.02 us
    add x1, other arithmetic, four_by_eight(): summed = keep + got.astype(F32)  0.98 us
  transfers between devices with their start and end apart: 12, of which 6 were waited for; matrix products, arithmetic and copies ran while one was open for 5% of the time, Pallas kernels for 5%

profile of v1, /device:TPU:0, one launch (start us, length us, event | category | flops | bytes accessed | tf_op | source)
XLA Modules:
  0.0 46.8 jit_solution(12876519242325947547)
XLA Ops:
  0.6 4.1 %collective-permute-start.1 = (bf16[128,512]{1,0:T(8,128)(2,1)}, bf16[128,512]{1,0:T(8,128)(2,1)S(1)}, u32[]{:S(2)}, u32[]{:S(2)}) collective-permute-start(bf16[128,512]{1,0:T(8,128)(2,1)} %f0.1), channel_id=1, source_target_pairs={{0,2},{1,3},{2,0},{3,1},{4,6},{5,7},{6,4},{7,5},{8,10},{9,11},{10,... | collective-permute-start | bytes 393224 | tf_op jit(solution)/shard_map/ppermute | solution.py:86
  4.7 1.6 %collective-permute-start = (bf16[128,512]{1,0:T(8,128)(2,1)}, bf16[128,512]{1,0:T(8,128)(2,1)S(1)}, u32[]{:S(2)}, u32[]{:S(2)}) collective-permute-start(bf16[128,512]{1,0:T(8,128)(2,1)} %f0.1), channel_id=1, source_target_pairs={{0,1},{1,0},{2,3},{3,2},{4,5},{5,4},{6,7},{7,6},{8,9},{9,8},{10,11... | collective-permute-start | bytes 393224 | tf_op jit(solution)/shard_map/ppermute | solution.py:86
  6.3 0.9 %collective-permute-start.4 = (bf16[128,512]{1,0:T(8,128)(2,1)}, bf16[128,512]{1,0:T(8,128)(2,1)S(1)}, u32[]{:S(2)}, u32[]{:S(2)}) collective-permute-start(bf16[128,512]{1,0:T(8,128)(2,1)} %ct0.1), channel_id=1, source_target_pairs={{0,1},{1,0},{2,3},{3,2},{4,5},{5,4},{6,7},{7,6},{8,9},{9,8},{10,11... | collective-permute-start | bytes 393224 | tf_op jit(solution)/shard_map/ppermute | solution.py:86
  7.9 0.6 %copy-done.7 = s32[1,2]{1,0:T(1,128)S(1)} copy-done((s32[1,2]{1,0:T(1,128)S(1)}, s32[1,2]{1,0:T(1,128)}, u32[]{:S(2)}) %copy-start.7) | copy-done | bytes 32
  8.7 0.9 %pad_maximum_fusion.1.tp0 = bf16[288,128]{1,0:T(8,128)(2,1)S(1)} fusion(bf16[256,128]{1,0:T(8,128)(2,1)} %bitcast.15, bf16[288]{0:T(512)(128)(2,1)S(1)} %pad.3.clone), kind=kLoop, calls=%fused_computation.8 | loop fusion | flops 147456 | bytes 139840 | tf_op jit(solution)/shard_map/concatenate | solution.py:156
  9.7 1.2 %collective-permute-start.3 = (bf16[288,128]{1,0:T(8,128)(2,1)S(1)}, bf16[288,128]{1,0:T(8,128)(2,1)S(1)}, u32[]{:S(2)}, u32[]{:S(2)}) collective-permute-start(bf16[288,128]{1,0:T(8,128)(2,1)S(1)} %pad_maximum_fusion.1.tp0), channel_id=1, source_target_pairs={{0,1},{1,0},{2,3},{3,2},{4,5},{5,4},{6,7},{7,6},{8,9},{9,8},{10,11... | collective-permute-start | bytes 221192 | tf_op jit(solution)/shard_map/ppermute | solution.py:86
  10.8 0.6 %pad_add_fusion.where = s32[2]{0:T(128)} fusion(s32[1]{0:T(128)} %bitcast.1, s32[1]{0:T(128)} %bitcast), kind=kLoop, calls=%fused_computation.14 | loop fusion | flops 2 | bytes 16 | tf_op jit(solution)/shard_map/stack | solution.py:158
  11.4 7.3 %collective-permute-done.3.tp1 = bf16[288,128]{1,0:T(8,128)(2,1)S(1)} collective-permute-done((bf16[288,128]{1,0:T(8,128)(2,1)S(1)}, bf16[288,128]{1,0:T(8,128)(2,1)S(1)}, u32[]{:S(2)}, u32[]{:S(2)}) %collective-permute-start.3) | collective-permute-done | bytes 73760 | tf_op jit(solution)/shard_map/ppermute | solution.py:86
  18.8 0.6 %copy-done.6 = bf16[288,128]{1,0:T(8,128)(2,1)} copy-done((bf16[288,128]{1,0:T(8,128)(2,1)}, bf16[288,128]{1,0:T(8,128)(2,1)S(1)}, u32[]{:S(2)}) %copy-start.6) | copy-done | bytes 73752
  19.5 0.7 %copy-done.4 = bf16[128,512]{1,0:T(8,128)(2,1)} copy-done((bf16[128,512]{1,0:T(8,128)(2,1)}, bf16[128,512]{1,0:T(8,128)(2,1)S(1)}, u32[]{:S(2)}) %copy-start.4) | copy-done | bytes 131096
  20.2 3.1 %shard_map.85 = (bf16[128,512]{1,0:T(8,128)(2,1)}, bf16[256,512]{1,0:T(8,128)(2,1)}, bf16[256,256]{1,0:T(8,128)(2,1)}, f32[2,64,512]{2,1,0:T(8,128)}, bf16[2,64,512]{2,1,0:T(8,128)(2,1)}) custom-call(s32[2]{0:T(128)} %pad_add_fusion.where, bf16[128,512]{1,0:T(8,128)(2,1)} %f0.1, bf16[128,512]{1,0:T(8,128)(2,1)} %copy-done.3, bf16[128,512]{1,0:T(8,128)(2,1)} %copy-done.2, ...), custom_call_target="tpu_custom_call" | custom-call | flops 402653184 | bytes 3145728 | tf_op jit(solution)/shard_map/pallas_call | solution.py:160
  23.2 1.6 %collective-permute-done.6 = bf16[2,64,512]{2,1,0:T(8,128)(2,1)S(1)} collective-permute-done((bf16[2,64,512]{2,1,0:T(8,128)(2,1)}, bf16[2,64,512]{2,1,0:T(8,128)(2,1)S(1)}, u32[]{:S(2)}, u32[]{:S(2)}) %collective-permute-start.6) | collective-permute-done | bytes 131104 | tf_op jit(solution)/shard_map/ppermute | solution.py:86
  24.8 1.0 %convert_add_fusion = f32[2,64,512]{2,1,0:T(8,128)S(1)} fusion(f32[2,64,512]{2,1,0:T(8,128)} %get-tuple-element.15, bf16[2,64,512]{2,1,0:T(8,128)(2,1)S(1)} %collective-permute-done.6), kind=kLoop, calls=%fused_computation.1 | loop fusion | flops 131072 | bytes 655360 | tf_op jit(solution)/shard_map/add | solution.py:181
  25.8 1.4 %collective-permute-start.7 = (bf16[64,512]{1,0:T(8,128)(2,1)S(1)}, bf16[64,512]{1,0:T(8,128)(2,1)S(1)}, u32[]{:S(2)}, u32[]{:S(2)}) collective-permute-start(bf16[64,512]{1,0:T(8,128)(2,1)S(1)} %fusion.2), channel_id=1, source_target_pairs={{0,2},{1,3},{2,0},{3,1},{4,6},{5,7},{6,4},{7,5},{8,10},{9,11},{10,... | collective-permute-start | bytes 196616 | tf_op jit(solution)/shard_map/ppermute | solution.py:86
  27.2 5.2 %collective-permute-done.7 = bf16[64,512]{1,0:T(8,128)(2,1)S(1)} collective-permute-done((bf16[64,512]{1,0:T(8,128)(2,1)S(1)}, bf16[64,512]{1,0:T(8,128)(2,1)S(1)}, u32[]{:S(2)}, u32[]{:S(2)}) %collective-permute-start.7) | collective-permute-done | bytes 65568 | tf_op jit(solution)/shard_map/ppermute | solution.py:86
  32.5 2.6 %collective-permute-start.10 = (bf16[64,512]{1,0:T(8,128)(2,1)S(1)}, bf16[64,512]{1,0:T(8,128)(2,1)S(1)}, u32[]{:S(2)}, u32[]{:S(2)}) collective-permute-start(bf16[64,512]{1,0:T(8,128)(2,1)S(1)} %fusion.1), channel_id=1, source_target_pairs={{0,24},{4,28},{8,16},{12,20},{16,8},{20,12},{24,0},{28,4},{1,25},{... | collective-permute-start | bytes 196616 | tf_op jit(solution)/shard_map/ppermute | solution.py:86
  35.0 0.5 %collective-permute-start.9 = (bf16[64,512]{1,0:T(8,128)(2,1)S(1)}, bf16[64,512]{1,0:T(8,128)(2,1)S(1)}, u32[]{:S(2)}, u32[]{:S(2)}) collective-permute-start(bf16[64,512]{1,0:T(8,128)(2,1)S(1)} %fusion.1), channel_id=1, source_target_pairs={{0,16},{4,20},{8,24},{12,28},{16,0},{20,4},{24,8},{28,12},{1,17},{... | collective-permute-start | bytes 196616 | tf_op jit(solution)/shard_map/ppermute | solution.py:86
  35.5 0.5 %collective-permute-start.8 = (bf16[64,512]{1,0:T(8,128)(2,1)S(1)}, bf16[64,512]{1,0:T(8,128)(2,1)S(1)}, u32[]{:S(2)}, u32[]{:S(2)}) collective-permute-start(bf16[64,512]{1,0:T(8,128)(2,1)S(1)} %fusion.1), channel_id=1, source_target_pairs={{0,8},{4,12},{8,0},{12,4},{16,24},{20,28},{24,16},{28,20},{1,9},{5... | collective-permute-start | bytes 196616 | tf_op jit(solution)/shard_map/ppermute | solution.py:86
  36.0 2.4 %shard_map.86 = (bf16[128,512]{1,0:T(8,128)(2,1)}, f32[128,512]{1,0:T(8,128)}) custom-call(bf16[256,512]{1,0:T(8,128)(2,1)} %get-tuple-element.11.gp, bf16[256,256]{1,0:T(8,128)(2,1)} %get-tuple-element.12.sel, bf16[512,512]{1,0:T(8,128)(2,1)} %w.3), custom_call_target="tpu_custom_call" | custom-call | flops 268435456 | bytes 2097152 | tf_op jit(solution)/shard_map/pallas_call | solution.py:184
  38.5 0.8 %collective-permute-done.9 = bf16[64,512]{1,0:T(8,128)(2,1)S(1)} collective-permute-done((bf16[64,512]{1,0:T(8,128)(2,1)S(1)}, bf16[64,512]{1,0:T(8,128)(2,1)S(1)}, u32[]{:S(2)}, u32[]{:S(2)}) %collective-permute-start.9) | collective-permute-done | bytes 65568 | tf_op jit(solution)/shard_map/ppermute | solution.py:86
  39.3 0.5 %collective-permute-done.8 = bf16[64,512]{1,0:T(8,128)(2,1)S(1)} collective-permute-done((bf16[64,512]{1,0:T(8,128)(2,1)S(1)}, bf16[64,512]{1,0:T(8,128)(2,1)S(1)}, u32[]{:S(2)}, u32[]{:S(2)}) %collective-permute-start.8) | collective-permute-done | bytes 65568 | tf_op jit(solution)/shard_map/ppermute | solution.py:86
  39.9 5.5 %collective-permute-done.5 = bf16[128,512]{1,0:T(8,128)(2,1)S(1)} collective-permute-done((bf16[128,512]{1,0:T(8,128)(2,1)}, bf16[128,512]{1,0:T(8,128)(2,1)S(1)}, u32[]{:S(2)}, u32[]{:S(2)}) %collective-permute-start.5) | collective-permute-done | bytes 131104 | tf_op jit(solution)/shard_map/ppermute | solution.py:86
  45.4 0.7 %add_convert_fusion = bf16[128,512]{1,0:T(8,128)(2,1)} fusion(f32[128,512]{1,0:T(8,128)S(1)} %copy-done, bf16[128,512]{1,0:T(8,128)(2,1)S(1)} %collective-permute-done.5), kind=kLoop, calls=%fused_computation.2 | loop fusion | flops 196608 | bytes 524288 | tf_op jit(solution)/shard_map/convert_element_type | solution.py:205
  46.1 0.7 %pad_maximum_fusion = f32[128,512]{1,0:T(8,128)} fusion(f32[64,512]{1,0:T(8,128)S(1)} %get-tuple-element.18, f32[64,512]{1,0:T(8,128)S(1)} %get-tuple-element.17), kind=kLoop, calls=%fused_computation | loop fusion | flops 65536 | bytes 524288 | tf_op jit(solution)/shard_map/concatenate | solution.py:204
  (31 shorter events, 0.5 us)
Async XLA Ops:
  0.6 18.1 %collective-permute-start.1 = (bf16[128,512]{1,0:T(8,128)(2,1)}, bf16[128,512]{1,0:T(8,128)(2,1)S(1)}, u32[]{:S(2)}, u32[]{:S(2)}) collective-permute-start(bf16[128,512]{1,0:T(8,128)(2,1)} %f0.1), channel_id=1, source_target_pairs={{0,2},{1,3},{2,0},{3,1},{4,6},{5,7},{6,4},{7,5},{8,10},{9,11},{10,... | collective-permute-start | bytes 393224 | tf_op jit(solution)/shard_map/ppermute | solution.py:86
  4.7 14.0 %collective-permute-start = (bf16[128,512]{1,0:T(8,128)(2,1)}, bf16[128,512]{1,0:T(8,128)(2,1)S(1)}, u32[]{:S(2)}, u32[]{:S(2)}) collective-permute-start(bf16[128,512]{1,0:T(8,128)(2,1)} %f0.1), channel_id=1, source_target_pairs={{0,1},{1,0},{2,3},{3,2},{4,5},{5,4},{6,7},{7,6},{8,9},{9,8},{10,11... | collective-permute-start | bytes 393224 | tf_op jit(solution)/shard_map/ppermute | solution.py:86
  6.3 12.5 %collective-permute-start.2 = (bf16[128,512]{1,0:T(8,128)(2,1)}, bf16[128,512]{1,0:T(8,128)(2,1)S(1)}, u32[]{:S(2)}, u32[]{:S(2)}) collective-permute-start(bf16[128,512]{1,0:T(8,128)(2,1)} %f0.1), channel_id=1, source_target_pairs={{0,3},{1,2},{2,1},{3,0},{4,7},{5,6},{6,5},{7,4},{8,11},{9,10},{10,... | collective-permute-start | bytes 393224 | tf_op jit(solution)/shard_map/ppermute | solution.py:86
  6.3 12.4 %collective-permute-start.4 = (bf16[128,512]{1,0:T(8,128)(2,1)}, bf16[128,512]{1,0:T(8,128)(2,1)S(1)}, u32[]{:S(2)}, u32[]{:S(2)}) collective-permute-start(bf16[128,512]{1,0:T(8,128)(2,1)} %ct0.1), channel_id=1, source_target_pairs={{0,1},{1,0},{2,3},{3,2},{4,5},{5,4},{6,7},{7,6},{8,9},{9,8},{10,11... | collective-permute-start | bytes 393224 | tf_op jit(solution)/shard_map/ppermute | solution.py:86
  7.9 0.7 %copy-start.7 = (s32[1,2]{1,0:T(1,128)S(1)}, s32[1,2]{1,0:T(1,128)}, u32[]{:S(2)}) copy-start(s32[1,2]{1,0:T(1,128)} %param.10) | copy-start | bytes 28
  9.6 9.2 %copy-start.1 = (bf16[288,128]{1,0:T(8,128)(2,1)}, bf16[288,128]{1,0:T(8,128)(2,1)S(1)}, u32[]{:S(2)}) copy-start(bf16[288,128]{1,0:T(8,128)(2,1)S(1)} %pad_maximum_fusion.1.tp0) | copy-start | bytes 221188
  9.7 9.1 %collective-permute-start.3 = (bf16[288,128]{1,0:T(8,128)(2,1)S(1)}, bf16[288,128]{1,0:T(8,128)(2,1)S(1)}, u32[]{:S(2)}, u32[]{:S(2)}) collective-permute-start(bf16[288,128]{1,0:T(8,128)(2,1)S(1)} %pad_maximum_fusion.1.tp0), channel_id=1, source_target_pairs={{0,1},{1,0},{2,3},{3,2},{4,5},{5,4},{6,7},{7,6},{8,9},{9,8},{10,11... | collective-permute-start | bytes 221192 | tf_op jit(solution)/shard_map/ppermute | solution.py:86
  18.7 0.6 %copy-start.6 = (bf16[288,128]{1,0:T(8,128)(2,1)}, bf16[288,128]{1,0:T(8,128)(2,1)S(1)}, u32[]{:S(2)}) copy-start(bf16[288,128]{1,0:T(8,128)(2,1)S(1)} %collective-permute-done.3.tp1) | copy-start | bytes 221188
  18.7 0.7 %copy-start.5 = (bf16[128,512]{1,0:T(8,128)(2,1)}, bf16[128,512]{1,0:T(8,128)(2,1)S(1)}, u32[]{:S(2)}) copy-start(bf16[128,512]{1,0:T(8,128)(2,1)S(1)} %collective-permute-done.4.ct1) | copy-start | bytes 393220
  18.8 0.7 %copy-start.2 = (bf16[128,512]{1,0:T(8,128)(2,1)}, bf16[128,512]{1,0:T(8,128)(2,1)S(1)}, u32[]{:S(2)}) copy-start(bf16[128,512]{1,0:T(8,128)(2,1)S(1)} %collective-permute-done.1.f2) | copy-start | bytes 393220
  18.8 0.7 %copy-start.3 = (bf16[128,512]{1,0:T(8,128)(2,1)}, bf16[128,512]{1,0:T(8,128)(2,1)S(1)}, u32[]{:S(2)}) copy-start(bf16[128,512]{1,0:T(8,128)(2,1)S(1)} %collective-permute-done.f1) | copy-start | bytes 393220
  19.5 0.7 %copy-start.4 = (bf16[128,512]{1,0:T(8,128)(2,1)}, bf16[128,512]{1,0:T(8,128)(2,1)S(1)}, u32[]{:S(2)}) copy-start(bf16[128,512]{1,0:T(8,128)(2,1)S(1)} %collective-permute-done.2.f3) | copy-start | bytes 393220
  23.2 1.6 %collective-permute-start.6 = (bf16[2,64,512]{2,1,0:T(8,128)(2,1)}, bf16[2,64,512]{2,1,0:T(8,128)(2,1)S(1)}, u32[]{:S(2)}, u32[]{:S(2)}) collective-permute-start(bf16[2,64,512]{2,1,0:T(8,128)(2,1)} %get-tuple-element.16), channel_id=1, source_target_pairs={{0,4},{4,0},{8,12},{12,8},{16,20},{20,16},{24,28},{28,24},{1,5},{5... | collective-permute-start | bytes 393224 | tf_op jit(solution)/shard_map/ppermute | solution.py:86
  25.8 6.6 %collective-permute-start.7 = (bf16[64,512]{1,0:T(8,128)(2,1)S(1)}, bf16[64,512]{1,0:T(8,128)(2,1)S(1)}, u32[]{:S(2)}, u32[]{:S(2)}) collective-permute-start(bf16[64,512]{1,0:T(8,128)(2,1)S(1)} %fusion.2), channel_id=1, source_target_pairs={{0,2},{1,3},{2,0},{3,1},{4,6},{5,7},{6,4},{7,5},{8,10},{9,11},{10,... | collective-permute-start | bytes 196616 | tf_op jit(solution)/shard_map/ppermute | solution.py:86
  32.5 6.0 %collective-permute-start.10 = (bf16[64,512]{1,0:T(8,128)(2,1)S(1)}, bf16[64,512]{1,0:T(8,128)(2,1)S(1)}, u32[]{:S(2)}, u32[]{:S(2)}) collective-permute-start(bf16[64,512]{1,0:T(8,128)(2,1)S(1)} %fusion.1), channel_id=1, source_target_pairs={{0,24},{4,28},{8,16},{12,20},{16,8},{20,12},{24,0},{28,4},{1,25},{... | collective-permute-start | bytes 196616 | tf_op jit(solution)/shard_map/ppermute | solution.py:86
  35.0 4.3 %collective-permute-start.9 = (bf16[64,512]{1,0:T(8,128)(2,1)S(1)}, bf16[64,512]{1,0:T(8,128)(2,1)S(1)}, u32[]{:S(2)}, u32[]{:S(2)}) collective-permute-start(bf16[64,512]{1,0:T(8,128)(2,1)S(1)} %fusion.1), channel_id=1, source_target_pairs={{0,16},{4,20},{8,24},{12,28},{16,0},{20,4},{24,8},{28,12},{1,17},{... | collective-permute-start | bytes 196616 | tf_op jit(solution)/shard_map/ppermute | solution.py:86
  35.5 4.3 %collective-permute-start.8 = (bf16[64,512]{1,0:T(8,128)(2,1)S(1)}, bf16[64,512]{1,0:T(8,128)(2,1)S(1)}, u32[]{:S(2)}, u32[]{:S(2)}) collective-permute-start(bf16[64,512]{1,0:T(8,128)(2,1)S(1)} %fusion.1), channel_id=1, source_target_pairs={{0,8},{4,12},{8,0},{12,4},{16,24},{20,28},{24,16},{28,20},{1,9},{5... | collective-permute-start | bytes 196616 | tf_op jit(solution)/shard_map/ppermute | solution.py:86
  38.4 7.0 %copy-start = (f32[128,512]{1,0:T(8,128)S(1)}, f32[128,512]{1,0:T(8,128)}, u32[]{:S(2)}) copy-start(f32[128,512]{1,0:T(8,128)} %get-tuple-element.13) | copy-start | bytes 786436
  38.5 7.0 %collective-permute-start.5 = (bf16[128,512]{1,0:T(8,128)(2,1)}, bf16[128,512]{1,0:T(8,128)(2,1)S(1)}, u32[]{:S(2)}, u32[]{:S(2)}) collective-permute-start(bf16[128,512]{1,0:T(8,128)(2,1)} %get-tuple-element.14), channel_id=1, source_target_pairs={{0,2},{1,3},{2,0},{3,1},{4,6},{5,7},{6,4},{7,5},{8,10},{9,11},{10,... | collective-permute-start | bytes 393224 | tf_op jit(solution)/shard_map/ppermute | solution.py:86
  39.8 6.3 %collective-permute-start.11 = (f32[64,512]{1,0:T(8,128)S(1)}, f32[64,512]{1,0:T(8,128)S(1)}, u32[]{:S(2)}, u32[]{:S(2)}) collective-permute-start(f32[64,512]{1,0:T(8,128)S(1)} %add_add_fusion), channel_id=1, source_target_pairs={{0,4},{4,0},{8,12},{12,8},{16,20},{20,16},{24,28},{28,24},{1,5},{5... | collective-permute-start | bytes 393224 | tf_op jit(solution)/shard_map/ppermute | solution.py:86

commit v2 on v1

--- a/solution.py
+++ b/solution.py
@@ -90,55 +90,88 @@
     return [pl.BlockSpec(memory_space=pltpu.VMEM)] * count
 
 
-def forward_kernel(scale, slots, where, f0, f1, f2, f3, tp0, tp1, ct0, ct1, w,
-                   out, gp, sel, keep, send, adj, agg, gw):
-    tile = f0.shape[0]
+def place(adj, row, tp, own, slots):
+    tile = tp.shape[1]
+    for t in range(4):
+        name = (own ^ t).astype(F32)
+        total = jnp.zeros((tile, tile), F32)
+        for s in range(slots):
+            mark = tp[pl.ds(slots * tile + 16 * s, 16), :][0:1, :].astype(F32)
+            block = tp[pl.ds(s * tile, tile), :]
+            total = total + jnp.where(mark == name, block.astype(F32), 0.0)
+        adj[pl.ds(row, tile), pl.ds(t * tile, tile)] = total.astype(BF16)
+
+
+def stage_kernel(slots, where, tp, f, ct, w, f_out, ct_out, w_out, adj):
+    place(adj, 0, tp, where[0], slots)
+    f_out[...] = f[...]
+    ct_out[...] = ct[...]
+    w_out[...] = w[...]
+
+
+def activate(adj, near, far, own_rows, ct, w):
+    half = near.shape[0]
+    summed = own_rows.astype(F32)
+    summed = summed + jnp.dot(adj[:, :half], near, preferred_element_type=F32)
+    summed = summed + jnp.dot(adj[:, half:], far, preferred_element_type=F32)
+    agg = summed.astype(BF16)
+    pre = jnp.dot(agg, w, preferred_element_type=F32)
+    sig = jax.nn.sigmoid(pre)
+    slope = ct.astype(F32) * sig * (1.0 + pre * (1.0 - sig))
+    return agg, (pre * sig).astype(BF16), slope.astype(BF16)
+
+
+def own_kernel(f0, f1, f2, f3, adj, ct, w, out, agg, gp, near, far):
+    tile = f1.shape[0]
+    near[:tile], near[tile:] = f0[...], f1[...]
+    far[:tile], far[tile:] = f2[...], f3[...]
+    agg[...], out[...], gp[...] = activate(adj[...], near[...], far[...], f0[...], ct[...], w[...])
+
+
+def pair_kernel(scale, slots, where, near, far, tp, ct, w, agg0, gp0,
+                gp1, adj, keep, send, agg, gp, gw):
+    tile = tp.shape[1]
     own, half = where[0], where[1]
-    for b, tp in enumerate((tp0, tp1)):
-        for t in range(4):
-            name = (own ^ t).astype(F32)
-            total = jnp.zeros((tile, tile), BF16)
-            for s in range(slots):
-                mark = tp[pl.ds(slots * tile + 16 * s, 16), :][0:1, :].astype(F32)
-                block = tp[pl.ds(s * tile, tile), :]
-                total = total + jnp.where(mark == name, block.astype(F32), 0.0).astype(BF16)
-            adj[pl.ds(b * tile, tile), pl.ds(t * tile, tile)] = total
-    near = jnp.concatenate([f0[...], f1[...]], axis=0)
-    far = jnp.concatenate([f2[...], f3[...]], axis=0)
-    summed = near.astype(F32)
-    summed = summed + jnp.dot(adj[:, : 2 * tile], near, preferred_element_type=F32)
-    summed = summed + jnp.dot(adj[:, 2 * tile :], far, preferred_element_type=F32)
-    agg[...] = summed.astype(BF16)
-    pre = jnp.dot(agg[...], w[...], preferred_element_type=F32)
-    sig = jax.nn.sigmoid(pre)
-    out[...] = (pre[:tile] * sig[:tile]).astype(BF16)
-    cot = jnp.concatenate([ct0[...], ct1[...]], axis=0).astype(F32)
-    gp[...] = (cot * sig * (1.0 + pre * (1.0 - sig))).astype(BF16)
-    sel[:, :tile] = adj[:, :tile]
-    sel[:, tile:] = adj[:, 2 * tile : 3 * tile]
+    place(adj, 0, tp, own, slots)
+    agg[:tile], gp[:tile] = agg0[...], gp0[...]
+    agg1, _, slope = activate(adj[...], near[...], far[...], near[tile:], ct[...], w[...])
+    agg[tile:], gp[tile:], gp1[...] = agg1, slope, slope
+    part = tile // 2
     for b in range(2):
         lane = pl.multiple_of((own ^ (2 * b)) * tile, tile)
         gw[pl.ds(b * tile, tile), :] = lax.dot_general(
             agg[:, pl.ds(lane, tile)], gp[...], (((0,), (0,)), ((), ())),
             preferred_element_type=F32,
         ) * scale
-        part = tile // 2
         mine = pl.multiple_of(b * tile + half * part, part)
         other = pl.multiple_of(b * tile + (1 - half) * part, part)
         keep[b] = gw[pl.ds(mine, part), :]
         send[b] = gw[pl.ds(other, part), :].astype(BF16)
 
 
-def backward_kernel(gp, sel, w, back, part):
-    tile = gp.shape[0] // 2
-    mid = lax.dot_general(
-        gp[...], w[...], (((1,), (1,)), ((), ())), preferred_element_type=F32
-    ).astype(BF16)
-    terms = lax.dot_general(
-        sel[...], mid, (((0,), (0,)), ((), ())), preferred_element_type=F32
-    )
+def pack_kernel(index, count, blocks, packed):
+    slots, tile, _ = blocks.shape
+    for s in range(slots):
+        packed[pl.ds(s * tile, tile), :] = blocks[s]
+        mark = jnp.where(s < count[0], index[0, s], -1).astype(F32)
+        packed[pl.ds(slots * tile + 16 * s, 16), :] = jnp.full((16, tile), mark, F32).astype(BF16)
+
+
+def backward_kernel(gp0, gp1, adj0, adj1, w, back, part):
+    tile = gp0.shape[0]
+    terms = jnp.zeros((2 * tile, w.shape[0]), F32)
+    for b, (gp, adj) in enumerate(((gp0, adj0), (gp1, adj1))):
+        mid = lax.dot_general(
+            gp[...], w[...], (((1,), (1,)), ((), ())), preferred_element_type=F32
+        ).astype(BF16)
+        sel = jnp.concatenate([adj[:, :tile], adj[:, 2 * tile : 3 * tile]], axis=1)
+        terms = terms + lax.dot_general(
+            sel, mid, (((0,), (0,)), ((), ())), preferred_element_type=F32
+        )
+        if b == 0:
+            part[...] = mid.astype(F32)
     back[...] = terms[tile:].astype(BF16)
-    part[...] = mid[:tile].astype(F32) + terms[:tile]
+    part[...] = part[...] + terms[:tile]
 
 
 def four_by_eight(features, weight, cotangent, tile_blocks, tile_index, tile_count):
@@ -146,40 +179,68 @@
     slots, tile, _ = tile_blocks.shape
     own = lax.axis_index("col")
     half = lax.axis_index("row") & 1
+    where = jnp.stack([own, half]).astype(jnp.int32)
     f3 = swap(features, "col", 3, 4)
     f2 = swap(features, "col", 2, 4)
     f1 = swap(features, "col", 1, 4)
     ct1 = swap(cotangent, "col", 1, 4)
-    live = jnp.arange(slots, dtype=jnp.int32) < tile_count[0]
-    marks = jnp.where(live, tile_index[0], -1).astype(BF16)
-    marks = jnp.broadcast_to(marks[:, None, None], (slots, 16, tile)).reshape(slots * 16, tile)
-    tp0 = jnp.concatenate([tile_blocks.reshape(slots * tile, tile), marks], axis=0)
+    tp0 = pl.pallas_call(
+        pack_kernel,
+        out_shape=jax.ShapeDtypeStruct((slots * (tile + 16), tile), BF16),
+        in_specs=[pl.BlockSpec(memory_space=pltpu.SMEM)] * 2 + vmem(1),
+        out_specs=vmem(1)[0],
+        compiler_params=pltpu.CompilerParams(vmem_limit_bytes=2 << 20),
+    )(tile_index, tile_count, tile_blocks)
     tp1 = swap(tp0, "col", 1, 4)
-    where = jnp.stack([own, half]).astype(jnp.int32)
-    scale = 1.0 / math.sqrt(rows * lax.axis_size("row") * lax.axis_size("col"))
-    out, gp, sel, keep, send = pl.pallas_call(
-        functools.partial(forward_kernel, scale, slots),
+    f0, ct0, w, adj0 = pl.pallas_call(
+        functools.partial(stage_kernel, slots),
         out_shape=(
             jax.ShapeDtypeStruct((rows, width), BF16),
-            jax.ShapeDtypeStruct((2 * rows, width), BF16),
-            jax.ShapeDtypeStruct((2 * rows, 2 * tile), BF16),
+            jax.ShapeDtypeStruct((rows, width), BF16),
+            jax.ShapeDtypeStruct((width, width), BF16),
+            jax.ShapeDtypeStruct((tile, 4 * tile), BF16),
+        ),
+        in_specs=[pl.BlockSpec(memory_space=pltpu.SMEM)] + vmem(4),
+        out_specs=tuple(vmem(4)),
+        compiler_params=pltpu.CompilerParams(vmem_limit_bytes=8 << 20),
+    )(where, tp0, features, cotangent, weight)
+    scale = 1.0 / math.sqrt(rows * lax.axis_size("row") * lax.axis_size("col"))
+    block = jax.ShapeDtypeStruct((rows, width), BF16)
+    double = jax.ShapeDtypeStruct((2 * rows, width), BF16)
+    out, agg0, gp0, near, far = pl.pallas_call(
+        own_kernel,
+        out_shape=(block, block, block, double, double),
+        in_specs=vmem(7),
+        out_specs=tuple(vmem(5)),
+        compiler_params=pltpu.CompilerParams(vmem_limit_bytes=8 << 20),
+        cost_estimate=pl.CostEstimate(
+            flops=4 * rows * width * width, bytes_accessed=1 << 20, transcendentals=rows * width
+        ),
+    )(f0, f1, f2, f3, adj0, ct0, w)
+    gp1, adj1, keep, send = pl.pallas_call(
+        functools.partial(pair_kernel, scale, slots),
+        out_shape=(
+            block,
+            jax.ShapeDtypeStruct((tile, 4 * tile), BF16),
             jax.ShapeDtypeStruct((2, tile // 2, width), F32),
             jax.ShapeDtypeStruct((2, tile // 2, width), BF16),
         ),
-        in_specs=[pl.BlockSpec(memory_space=pltpu.SMEM)] + vmem(9),
-        out_specs=tuple(vmem(5)),
+        in_specs=[pl.BlockSpec(memory_space=pltpu.SMEM)] + vmem(7),
+        out_specs=tuple(vmem(4)),
         scratch_shapes=[
-            pltpu.VMEM((2 * tile, 4 * tile), BF16),
+            pltpu.VMEM((2 * tile, width), BF16),
             pltpu.VMEM((2 * tile, width), BF16),
             pltpu.VMEM((2 * tile, width), F32),
         ],
+        compiler_params=pltpu.CompilerParams(vmem_limit_bytes=12 << 20),
         cost_estimate=pl.CostEstimate(
-            flops=2 * 256 * 512 * 512 * 3, bytes_accessed=3 << 20, transcendentals=256 * 512
-        ),
-    )(where, features, f1, f2, f3, tp0, tp1, cotangent, ct1, weight)
+            flops=8 * rows * width * width, bytes_accessed=2 << 20, transcendentals=rows * width
+        ),
+    )(where, near, far, tp1, ct1, w, agg0, gp0)
     got = swap(send, "row", 1, 8)
     summed = keep + got.astype(F32)
-    got = swap(summed[1].astype(BF16), "col", 2, 4)
+    pair_term, gp1 = lax.optimization_barrier((summed[1].astype(BF16), gp1))
+    got = swap(pair_term, "col", 2, 4)
     mine = (summed[0] + got.astype(F32)).astype(BF16)
     back, part = pl.pallas_call(
         backward_kernel,
@@ -187,22 +248,25 @@
             jax.ShapeDtypeStruct((rows, width), BF16),
             jax.ShapeDtypeStruct((rows, width), F32),
         ),
-        in_specs=vmem(3),
+        in_specs=vmem(5),
         out_specs=tuple(vmem(2)),
+        compiler_params=pltpu.CompilerParams(vmem_limit_bytes=12 << 20),
         cost_estimate=pl.CostEstimate(
             flops=2 * 256 * 512 * 512 * 2, bytes_accessed=2 << 20, transcendentals=0
         ),
-    )(gp, sel, weight)
+    )(gp0, gp1, adj0, adj1, w)
     got_back = swap(back, "col", 2, 4)
+    mine, back = lax.optimization_barrier((mine, back))
     diagonal = swap(mine, "row", 6, 8).astype(F32)
     along = swap(mine, "row", 4, 8).astype(F32)
     across = swap(mine, "row", 2, 8).astype(F32)
+    grad_features = (part + got_back.astype(F32)).astype(BF16)
+    along, grad_features = lax.optimization_barrier((along, grad_features))
     total = (mine.astype(F32) + across) + (along + diagonal)
     rest = swap(total, "row", 1, 8)
     first = jnp.where(half == 0, total, rest)
     second = jnp.where(half == 0, rest, total)
     grad_weight = jnp.concatenate([first, second], axis=0)
-    grad_features = (part + got_back.astype(F32)).astype(BF16)
     return (out, grad_features, grad_weight)
 
 

time: 47.1 us -> 38.6 us (0.82)
  waiting for transfers between devices: 20.9 us -> 13 us
  other arithmetic: 4 us -> 1.58 us
  starting transfers between devices: 12.8 us -> 14.5 us
  local copies, waits for them, and re-layouts: 2.2 us -> 3.45 us
  Pallas kernels: 5.51 us -> 4.28 us
    ppermute x12, waiting for transfers between devices: 20.9 us -> 13 us  [swap(): return lax.ppermute(value, axis, [(i, i ^ mask) for i in range(size)])]
    pallas_call x1, Pallas kernels: 2.43 us -> 0.75 us  [four_by_eight(): pl.pallas_call(backward_kernel, out_shape=(jax.ShapeDtypeStruct((rows, wi...]
    ppermute x12, starting transfers between devices: 12.8 us -> 14.5 us  [swap(): return lax.ppermute(value, axis, [(i, i ^ mask) for i in range(size)])]
    unnamed x16 -> x10, local copies, waits for them, and re-layouts: 2.02 us -> 3.44 us
    add x1, other arithmetic: 0.98 us -> 0.03 us  [four_by_eight(): summed = keep + got.astype(F32)]
    concatenate x1 -> x0, other arithmetic: 0.94 us -> none  [four_by_eight(): jnp.concatenate([tile_blocks.reshape(slots * tile, tile), marks], axis=0)]
    another operation x1, other arithmetic: 0.6 us -> 0.07 us  [four_by_eight(): where = jnp.stack([own, half]).astype(jnp.int32)]
    pallas_call x1 -> x4, Pallas kernels: 3.08 us -> 3.53 us  [the longest x1 1.24 us: four_by_eight(): pl.pallas_call(functools.partial(pair_kernel, scale, slots), out_shape=(b...]
  transfers between devices with their start and end apart: 12 -> 12, of which waited for: 6 -> 6; matrix products, arithmetic and copies ran while one was open for 5% -> 2% of each run, Pallas kernels for 5% -> 8%
where the time goes in v2:
time: 38.6 us; the launch traced here: 38.3 us
  starting transfers between devices  14.5 us (38%)
  waiting for transfers between devices  13 us (34%)
  Pallas kernels  4.28 us (11%)
  local copies, waits for them, and re-layouts  3.45 us (9%)
  other arithmetic  1.58 us (4%)
  between operations  1.43 us (4%)
    ppermute x12, starting transfers between devices, swap(): return lax.ppermute(value, axis, [(i, i ^ mask) for i in range(size)])  14.5 us
    ppermute x12, waiting for transfers between devices, swap(): return lax.ppermute(value, axis, [(i, i ^ mask) for i in range(size)])  13 us
    unnamed x10, local copies, waits for them, and re-layouts  3.44 us
    pallas_call x1, Pallas kernels, four_by_eight(): pl.pallas_call(functools.partial(pair_kernel, scale, slots), out_shape=(b...  1.24 us
    pallas_call x1, Pallas kernels, four_by_eight(): pl.pallas_call(own_kernel, out_shape=(block, block, block, double, double...  1.13 us
  transfers between devices with their start and end apart: 12, of which 6 were waited for; matrix products, arithmetic and copies ran while one was open for 2% of the time, Pallas kernels for 8%

profile of v2, /device:TPU:0, one launch (start us, length us, event | category | flops | bytes accessed | tf_op | source)
XLA Modules:
  0.0 38.3 jit_solution(13115032060967001867)
XLA Ops:
  0.6 3.1 %collective-permute-start = (bf16[128,512]{1,0:T(8,128)(2,1)}, bf16[128,512]{1,0:T(8,128)(2,1)S(1)}, u32[]{:S(2)}, u32[]{:S(2)}) collective-permute-start(bf16[128,512]{1,0:T(8,128)(2,1)} %f.1), channel_id=1, source_target_pairs={{0,1},{1,0},{2,3},{3,2},{4,5},{5,4},{6,7},{7,6},{8,9},{9,8},{10,11... | collective-permute-start | bytes 393224 | tf_op jit(solution)/shard_map/ppermute | solution.py:86
  3.7 2.5 %collective-permute-start.2 = (bf16[128,512]{1,0:T(8,128)(2,1)}, bf16[128,512]{1,0:T(8,128)(2,1)S(1)}, u32[]{:S(2)}, u32[]{:S(2)}) collective-permute-start(bf16[128,512]{1,0:T(8,128)(2,1)} %f.1), channel_id=1, source_target_pairs={{0,3},{1,2},{2,1},{3,0},{4,7},{5,6},{6,5},{7,4},{8,11},{9,10},{10,... | collective-permute-start | bytes 393224 | tf_op jit(solution)/shard_map/ppermute | solution.py:86
  6.3 1.8 %collective-permute-start.4 = (bf16[128,512]{1,0:T(8,128)(2,1)}, bf16[128,512]{1,0:T(8,128)(2,1)S(1)}, u32[]{:S(2)}, u32[]{:S(2)}) collective-permute-start(bf16[128,512]{1,0:T(8,128)(2,1)} %ct.1), channel_id=1, source_target_pairs={{0,1},{1,0},{2,3},{3,2},{4,5},{5,4},{6,7},{7,6},{8,9},{9,8},{10,11... | collective-permute-start | bytes 393224 | tf_op jit(solution)/shard_map/ppermute | solution.py:86
  8.8 0.8 %copy-done.3 = bf16[2,128,128]{2,1,0:T(8,128)(2,1)S(1)} copy-done((bf16[2,128,128]{2,1,0:T(8,128)(2,1)S(1)}, bf16[2,128,128]{2,1,0:T(8,128)(2,1)}, u32[]{:S(2)}) %copy-start.3) | copy-done | bytes 65560
  9.6 0.7 %copy-done.4 = s32[1,2]{1,0:T(1,128)S(1)} copy-done((s32[1,2]{1,0:T(1,128)S(1)}, s32[1,2]{1,0:T(1,128)}, u32[]{:S(2)}) %copy-start.4) | copy-done | bytes 32
  10.3 0.5 %shard_map.85.tp = bf16[288,128]{1,0:T(8,128)(2,1)S(1)} custom-call(s32[1,2]{1,0:T(1,128)S(1)} %copy-done.4, s32[1]{0:T(128)S(6)} %copy.9.count, bf16[2,128,128]{2,1,0:T(8,128)(2,1)S(1)} %copy-done.3), custom_call_target="tpu_custom_call" | custom-call | tf_op jit(solution)/shard_map/pallas_call | solution.py:187
  11.2 1.0 %copy-done = bf16[512,512]{1,0:T(8,128)(2,1)S(1)} copy-done((bf16[512,512]{1,0:T(8,128)(2,1)S(1)}, bf16[512,512]{1,0:T(8,128)(2,1)}, u32[]{:S(2)}) %copy-start) | copy-done | bytes 524312
  12.2 0.9 %copy-done.2 = bf16[128,512]{1,0:T(8,128)(2,1)S(1)} copy-done((bf16[128,512]{1,0:T(8,128)(2,1)S(1)}, bf16[128,512]{1,0:T(8,128)(2,1)}, u32[]{:S(2)}) %copy-start.2) | copy-done | bytes 131096
  13.1 0.6 %shard_map.86 = (bf16[128,512]{1,0:T(8,128)(2,1)S(1)}, bf16[128,512]{1,0:T(8,128)(2,1)S(1)}, bf16[512,512]{1,0:T(8,128)(2,1)S(1)}, bf16[128,512]{1,0:T(8,128)(2,1)S(1)}) custom-call(s32[2]{0:T(128)S(1)} %pad_add_fusion.where, bf16[288,128]{1,0:T(8,128)(2,1)S(1)} %shard_map.85.tp, bf16[128,512]{1,0:T(8,128)(2,1)S(1)} %copy-done.1, ...), custom_call_target="tpu_custom_call" | custom-call | tf_op jit(solution)/shard_map/pallas_call | solution.py:195
  13.8 4.5 %collective-permute-done.1.f2 = bf16[128,512]{1,0:T(8,128)(2,1)S(1)} collective-permute-done((bf16[128,512]{1,0:T(8,128)(2,1)}, bf16[128,512]{1,0:T(8,128)(2,1)S(1)}, u32[]{:S(2)}, u32[]{:S(2)}) %collective-permute-start.1) | collective-permute-done | bytes 131104 | tf_op jit(solution)/shard_map/ppermute | solution.py:86
  18.3 1.1 %shard_map.87 = (bf16[128,512]{1,0:T(8,128)(2,1)}, bf16[128,512]{1,0:T(8,128)(2,1)S(1)}, bf16[128,512]{1,0:T(8,128)(2,1)S(1)}, bf16[256,512]{1,0:T(8,128)(2,1)S(1)}, bf16[256,512]{1,0:T(8,128)(2,1)S(1)}) custom-call(bf16[128,512]{1,0:T(8,128)(2,1)S(1)} %get-tuple-element.23.f0, bf16[128,512]{1,0:T(8,128)(2,1)S(1)} %collective-permute-done.f1, ...), custom_call_target="tpu_custom_call" | custom-call | flops 134217728 | bytes 1048576 | tf_op jit(solution)/shard_map/pallas_call | solution.py:210
  19.4 1.2 %shard_map.88 = (bf16[128,512]{1,0:T(8,128)(2,1)S(1)}, bf16[128,512]{1,0:T(8,128)(2,1)S(1)}, f32[2,64,512]{2,1,0:T(8,128)S(1)}, bf16[2,64,512]{2,1,0:T(8,128)(2,1)S(1)}) custom-call(s32[2]{0:T(128)S(1)} %pad_add_fusion.where, bf16[256,512]{1,0:T(8,128)(2,1)S(1)} %get-tuple-element.28.near, bf16[256,512]{1,0:T(8,128)(2,1)S(1)} %get-tuple-element.29.far, ...), custom_call_target="tpu_custom_call" | custom-call | flops 268435456 | bytes 2097152 | tf_op jit(solution)/shard_map/pallas_call | solution.py:220
  20.8 1.3 %collective-permute-done.5 = bf16[2,64,512]{2,1,0:T(8,128)(2,1)S(1)} collective-permute-done((bf16[2,64,512]{2,1,0:T(8,128)(2,1)S(1)}, bf16[2,64,512]{2,1,0:T(8,128)(2,1)S(1)}, u32[]{:S(2)}, u32[]{:S(2)}) %collective-permute-start.5) | collective-permute-done | bytes 131104 | tf_op jit(solution)/shard_map/ppermute | solution.py:86
  22.2 0.9 %collective-permute-start.6 = (bf16[64,512]{1,0:T(8,128)(2,1)S(1)}, bf16[64,512]{1,0:T(8,128)(2,1)S(1)}, u32[]{:S(2)}, u32[]{:S(2)}) collective-permute-start(bf16[64,512]{1,0:T(8,128)(2,1)S(1)} %fusion.2), channel_id=1, source_target_pairs={{0,2},{1,3},{2,0},{3,1},{4,6},{5,7},{6,4},{7,5},{8,10},{9,11},{10,... | collective-permute-start | bytes 196616 | tf_op jit(solution)/shard_map/ppermute | solution.py:86
  23.0 0.7 %shard_map.89 = (bf16[128,512]{1,0:T(8,128)(2,1)S(1)}, f32[128,512]{1,0:T(8,128)S(1)}) custom-call(bf16[128,512]{1,0:T(8,128)(2,1)S(1)} %get-tuple-element.31.gp0, bf16[128,512]{1,0:T(8,128)(2,1)S(1)} %get-tuple-element.36.gp1, bf16[128,512]{1,0:T(8,128)(2,1)S(1)} %get-tuple-element.24.adj.adj0, bf16[128,512]{1,0:T(8,128)(2,1)S(1)} %get-tuple-element.37.adj1, ...), custom_call_target="tpu_custom_call" | custom-call | flops 268435456 | bytes 2097152 | tf_op jit(solution)/shard_map/pallas_call | solution.py:245
  23.8 2.2 %collective-permute-start.8 = (bf16[128,512]{1,0:T(8,128)(2,1)S(1)}, bf16[128,512]{1,0:T(8,128)(2,1)S(1)}, u32[]{:S(2)}, u32[]{:S(2)}) collective-permute-start(bf16[128,512]{1,0:T(8,128)(2,1)S(1)} %get-tuple-element.38), channel_id=1, source_target_pairs={{0,2},{1,3},{2,0},{3,1},{4,6},{5,7},{6,4},{7,5},{8,10},{9,11},{10,... | collective-permute-start | bytes 393224 | tf_op jit(solution)/shard_map/ppermute | solution.py:86
  26.0 2.7 %collective-permute-done.6 = bf16[64,512]{1,0:T(8,128)(2,1)S(1)} collective-permute-done((bf16[64,512]{1,0:T(8,128)(2,1)S(1)}, bf16[64,512]{1,0:T(8,128)(2,1)S(1)}, u32[]{:S(2)}, u32[]{:S(2)}) %collective-permute-start.6) | collective-permute-done | bytes 65568 | tf_op jit(solution)/shard_map/ppermute | solution.py:86
  28.7 2.5 %collective-permute-start.10 = (bf16[64,512]{1,0:T(8,128)(2,1)S(1)}, bf16[64,512]{1,0:T(8,128)(2,1)S(1)}, u32[]{:S(2)}, u32[]{:S(2)}) collective-permute-start(bf16[64,512]{1,0:T(8,128)(2,1)S(1)} %fusion.1), channel_id=1, source_target_pairs={{0,24},{4,28},{8,16},{12,20},{16,8},{20,12},{24,0},{28,4},{1,25},{... | collective-permute-start | bytes 196616 | tf_op jit(solution)/shard_map/ppermute | solution.py:86
  31.2 0.5 %collective-permute-start.9 = (bf16[64,512]{1,0:T(8,128)(2,1)S(1)}, bf16[64,512]{1,0:T(8,128)(2,1)S(1)}, u32[]{:S(2)}, u32[]{:S(2)}) collective-permute-start(bf16[64,512]{1,0:T(8,128)(2,1)S(1)} %fusion.1), channel_id=1, source_target_pairs={{0,8},{4,12},{8,0},{12,4},{16,24},{20,28},{24,16},{28,20},{1,9},{5... | collective-permute-start | bytes 196616 | tf_op jit(solution)/shard_map/ppermute | solution.py:86
  32.3 2.0 %collective-permute-done.8 = bf16[128,512]{1,0:T(8,128)(2,1)S(1)} collective-permute-done((bf16[128,512]{1,0:T(8,128)(2,1)S(1)}, bf16[128,512]{1,0:T(8,128)(2,1)S(1)}, u32[]{:S(2)}, u32[]{:S(2)}) %collective-permute-start.8) | collective-permute-done | bytes 131104 | tf_op jit(solution)/shard_map/ppermute | solution.py:86
  34.3 0.7 %add_convert_fusion = bf16[128,512]{1,0:T(8,128)(2,1)} fusion(f32[128,512]{1,0:T(8,128)S(1)} %get-tuple-element.40, bf16[128,512]{1,0:T(8,128)(2,1)S(1)} %collective-permute-done.8), kind=kLoop, calls=%fused_computation.1 | loop fusion | flops 196608 | bytes 524288 | tf_op jit(solution)/shard_map/convert_element_type | solution.py:263
  34.9 1.1 %collective-permute-done.7 = bf16[64,512]{1,0:T(8,128)(2,1)S(1)} collective-permute-done((bf16[64,512]{1,0:T(8,128)(2,1)S(1)}, bf16[64,512]{1,0:T(8,128)(2,1)S(1)}, u32[]{:S(2)}, u32[]{:S(2)}) %collective-permute-start.7) | collective-permute-done | bytes 65568 | tf_op jit(solution)/shard_map/ppermute | solution.py:86
  36.2 1.3 %collective-permute-done.11 = f32[64,512]{1,0:T(8,128)S(1)} collective-permute-done((f32[64,512]{1,0:T(8,128)S(1)}, f32[64,512]{1,0:T(8,128)S(1)}, u32[]{:S(2)}, u32[]{:S(2)}) %collective-permute-start.11) | collective-permute-done | bytes 131104 | tf_op jit(solution)/shard_map/ppermute | solution.py:86
  37.6 0.7 %pad_maximum_fusion = f32[128,512]{1,0:T(8,128)} fusion(f32[64,512]{1,0:T(8,128)S(1)} %get-tuple-element.44, f32[64,512]{1,0:T(8,128)S(1)} %get-tuple-element.43), kind=kLoop, calls=%fused_computation | loop fusion | flops 65536 | bytes 524288 | tf_op jit(solution)/shard_map/concatenate | solution.py:269
  (24 shorter events, 1.3 us)
Async XLA Ops:
  0.6 10.6 %copy-start.1 = (bf16[128,512]{1,0:T(8,128)(2,1)S(1)}, bf16[128,512]{1,0:T(8,128)(2,1)}, u32[]{:S(2)}) copy-start(bf16[128,512]{1,0:T(8,128)(2,1)} %f.1) | copy-start | bytes 393220
  0.6 13.1 %collective-permute-start = (bf16[128,512]{1,0:T(8,128)(2,1)}, bf16[128,512]{1,0:T(8,128)(2,1)S(1)}, u32[]{:S(2)}, u32[]{:S(2)}) collective-permute-start(bf16[128,512]{1,0:T(8,128)(2,1)} %f.1), channel_id=1, source_target_pairs={{0,1},{1,0},{2,3},{3,2},{4,5},{5,4},{6,7},{7,6},{8,9},{9,8},{10,11... | collective-permute-start | bytes 393224 | tf_op jit(solution)/shard_map/ppermute | solution.py:86
  3.7 10.0 %collective-permute-start.2 = (bf16[128,512]{1,0:T(8,128)(2,1)}, bf16[128,512]{1,0:T(8,128)(2,1)S(1)}, u32[]{:S(2)}, u32[]{:S(2)}) collective-permute-start(bf16[128,512]{1,0:T(8,128)(2,1)} %f.1), channel_id=1, source_target_pairs={{0,3},{1,2},{2,1},{3,0},{4,7},{5,6},{6,5},{7,4},{8,11},{9,10},{10,... | collective-permute-start | bytes 393224 | tf_op jit(solution)/shard_map/ppermute | solution.py:86
  6.2 12.1 %collective-permute-start.1 = (bf16[128,512]{1,0:T(8,128)(2,1)}, bf16[128,512]{1,0:T(8,128)(2,1)S(1)}, u32[]{:S(2)}, u32[]{:S(2)}) collective-permute-start(bf16[128,512]{1,0:T(8,128)(2,1)} %f.1), channel_id=1, source_target_pairs={{0,2},{1,3},{2,0},{3,1},{4,6},{5,7},{6,4},{7,5},{8,10},{9,11},{10,... | collective-permute-start | bytes 393224 | tf_op jit(solution)/shard_map/ppermute | solution.py:86
  6.3 13.1 %collective-permute-start.4 = (bf16[128,512]{1,0:T(8,128)(2,1)}, bf16[128,512]{1,0:T(8,128)(2,1)S(1)}, u32[]{:S(2)}, u32[]{:S(2)}) collective-permute-start(bf16[128,512]{1,0:T(8,128)(2,1)} %ct.1), channel_id=1, source_target_pairs={{0,1},{1,0},{2,3},{3,2},{4,5},{5,4},{6,7},{7,6},{8,9},{9,8},{10,11... | collective-permute-start | bytes 393224 | tf_op jit(solution)/shard_map/ppermute | solution.py:86
  8.8 0.8 %copy-start.3 = (bf16[2,128,128]{2,1,0:T(8,128)(2,1)S(1)}, bf16[2,128,128]{2,1,0:T(8,128)(2,1)}, u32[]{:S(2)}) copy-start(bf16[2,128,128]{2,1,0:T(8,128)(2,1)} %blocks.1) | copy-start | bytes 196612
  9.6 0.7 %copy-start.4 = (s32[1,2]{1,0:T(1,128)S(1)}, s32[1,2]{1,0:T(1,128)}, u32[]{:S(2)}) copy-start(s32[1,2]{1,0:T(1,128)} %index.1) | copy-start | bytes 28
  10.8 8.6 %collective-permute-start.3 = (bf16[288,128]{1,0:T(8,128)(2,1)S(1)}, bf16[288,128]{1,0:T(8,128)(2,1)S(1)}, u32[]{:S(2)}, u32[]{:S(2)}) collective-permute-start(bf16[288,128]{1,0:T(8,128)(2,1)S(1)} %shard_map.85.tp), channel_id=1, source_target_pairs={{0,1},{1,0},{2,3},{3,2},{4,5},{5,4},{6,7},{7,6},{8,9},{9,8},{10,11... | collective-permute-start | bytes 221192 | tf_op jit(solution)/shard_map/ppermute | solution.py:86
  11.2 1.0 %copy-start = (bf16[512,512]{1,0:T(8,128)(2,1)S(1)}, bf16[512,512]{1,0:T(8,128)(2,1)}, u32[]{:S(2)}) copy-start(bf16[512,512]{1,0:T(8,128)(2,1)} %w.1) | copy-start | bytes 1572868
  12.2 0.9 %copy-start.2 = (bf16[128,512]{1,0:T(8,128)(2,1)S(1)}, bf16[128,512]{1,0:T(8,128)(2,1)}, u32[]{:S(2)}) copy-start(bf16[128,512]{1,0:T(8,128)(2,1)} %ct.1) | copy-start | bytes 393220
  20.7 1.4 %collective-permute-start.5 = (bf16[2,64,512]{2,1,0:T(8,128)(2,1)S(1)}, bf16[2,64,512]{2,1,0:T(8,128)(2,1)S(1)}, u32[]{:S(2)}, u32[]{:S(2)}) collective-permute-start(bf16[2,64,512]{2,1,0:T(8,128)(2,1)S(1)} %get-tuple-element.33), channel_id=1, source_target_pairs={{0,4},{4,0},{8,12},{12,8},{16,20},{20,16},{24,28},{28,24},{1,5},{5... | collective-permute-start | bytes 393224 | tf_op jit(solution)/shard_map/ppermute | solution.py:86
  22.2 6.6 %collective-permute-start.6 = (bf16[64,512]{1,0:T(8,128)(2,1)S(1)}, bf16[64,512]{1,0:T(8,128)(2,1)S(1)}, u32[]{:S(2)}, u32[]{:S(2)}) collective-permute-start(bf16[64,512]{1,0:T(8,128)(2,1)S(1)} %fusion.2), channel_id=1, source_target_pairs={{0,2},{1,3},{2,0},{3,1},{4,6},{5,7},{6,4},{7,5},{8,10},{9,11},{10,... | collective-permute-start | bytes 196616 | tf_op jit(solution)/shard_map/ppermute | solution.py:86
  23.8 10.5 %collective-permute-start.8 = (bf16[128,512]{1,0:T(8,128)(2,1)S(1)}, bf16[128,512]{1,0:T(8,128)(2,1)S(1)}, u32[]{:S(2)}, u32[]{:S(2)}) collective-permute-start(bf16[128,512]{1,0:T(8,128)(2,1)S(1)} %get-tuple-element.38), channel_id=1, source_target_pairs={{0,2},{1,3},{2,0},{3,1},{4,6},{5,7},{6,4},{7,5},{8,10},{9,11},{10,... | collective-permute-start | bytes 393224 | tf_op jit(solution)/shard_map/ppermute | solution.py:86
  28.7 7.3 %collective-permute-start.10 = (bf16[64,512]{1,0:T(8,128)(2,1)S(1)}, bf16[64,512]{1,0:T(8,128)(2,1)S(1)}, u32[]{:S(2)}, u32[]{:S(2)}) collective-permute-start(bf16[64,512]{1,0:T(8,128)(2,1)S(1)} %fusion.1), channel_id=1, source_target_pairs={{0,24},{4,28},{8,16},{12,20},{16,8},{20,12},{24,0},{28,4},{1,25},{... | collective-permute-start | bytes 196616 | tf_op jit(solution)/shard_map/ppermute | solution.py:86
  31.2 4.8 %collective-permute-start.9 = (bf16[64,512]{1,0:T(8,128)(2,1)S(1)}, bf16[64,512]{1,0:T(8,128)(2,1)S(1)}, u32[]{:S(2)}, u32[]{:S(2)}) collective-permute-start(bf16[64,512]{1,0:T(8,128)(2,1)S(1)} %fusion.1), channel_id=1, source_target_pairs={{0,8},{4,12},{8,0},{12,4},{16,24},{20,28},{24,16},{28,20},{1,9},{5... | collective-permute-start | bytes 196616 | tf_op jit(solution)/shard_map/ppermute | solution.py:86
  31.8 4.3 %collective-permute-start.7 = (bf16[64,512]{1,0:T(8,128)(2,1)S(1)}, bf16[64,512]{1,0:T(8,128)(2,1)S(1)}, u32[]{:S(2)}, u32[]{:S(2)}) collective-permute-start(bf16[64,512]{1,0:T(8,128)(2,1)S(1)} %fusion.1), channel_id=1, source_target_pairs={{0,16},{4,20},{8,24},{12,28},{16,0},{20,4},{24,8},{28,12},{1,17},{... | collective-permute-start | bytes 196616 | tf_op jit(solution)/shard_map/ppermute | solution.py:86
  36.1 1.4 %collective-permute-start.11 = (f32[64,512]{1,0:T(8,128)S(1)}, f32[64,512]{1,0:T(8,128)S(1)}, u32[]{:S(2)}, u32[]{:S(2)}) collective-permute-start(f32[64,512]{1,0:T(8,128)S(1)} %add_add_fusion), channel_id=1, source_target_pairs={{0,4},{4,0},{8,12},{12,8},{16,20},{20,16},{24,28},{28,24},{1,5},{5... | collective-permute-start | bytes 393224 | tf_op jit(solution)/shard_map/ppermute | solution.py:86

commit v3 on v2

--- a/solution.py
+++ b/solution.py
@@ -118,14 +118,14 @@
     pre = jnp.dot(agg, w, preferred_element_type=F32)
     sig = jax.nn.sigmoid(pre)
     slope = ct.astype(F32) * sig * (1.0 + pre * (1.0 - sig))
-    return agg, (pre * sig).astype(BF16), slope.astype(BF16)
-
-
-def own_kernel(f0, f1, f2, f3, adj, ct, w, out, agg, gp, near, far):
+    return agg, pre, slope.astype(BF16)
+
+
+def own_kernel(f1, f2, f3, f0, adj, ct, w, pre, agg, gp, near, far):
     tile = f1.shape[0]
     near[:tile], near[tile:] = f0[...], f1[...]
     far[:tile], far[tile:] = f2[...], f3[...]
-    agg[...], out[...], gp[...] = activate(adj[...], near[...], far[...], f0[...], ct[...], w[...])
+    agg[...], pre[...], gp[...] = activate(adj[...], near[...], far[...], f0[...], ct[...], w[...])
 
 
 def pair_kernel(scale, slots, where, near, far, tp, ct, w, agg0, gp0,
@@ -207,16 +207,16 @@
     scale = 1.0 / math.sqrt(rows * lax.axis_size("row") * lax.axis_size("col"))
     block = jax.ShapeDtypeStruct((rows, width), BF16)
     double = jax.ShapeDtypeStruct((2 * rows, width), BF16)
-    out, agg0, gp0, near, far = pl.pallas_call(
+    pre, agg0, gp0, near, far = pl.pallas_call(
         own_kernel,
-        out_shape=(block, block, block, double, double),
+        out_shape=(jax.ShapeDtypeStruct((rows, width), F32), block, block, double, double),
         in_specs=vmem(7),
         out_specs=tuple(vmem(5)),
         compiler_params=pltpu.CompilerParams(vmem_limit_bytes=8 << 20),
         cost_estimate=pl.CostEstimate(
             flops=4 * rows * width * width, bytes_accessed=1 << 20, transcendentals=rows * width
         ),
-    )(f0, f1, f2, f3, adj0, ct0, w)
+    )(f1, f2, f3, f0, adj0, ct0, w)
     gp1, adj1, keep, send = pl.pallas_call(
         functools.partial(pair_kernel, scale, slots),
         out_shape=(
@@ -255,12 +255,14 @@
             flops=2 * 256 * 512 * 512 * 2, bytes_accessed=2 << 20, transcendentals=0
         ),
     )(gp0, gp1, adj0, adj1, w)
-    got_back = swap(back, "col", 2, 4)
+    odd = lax.ppermute(back, "col", [(1, 3), (3, 1)])
+    even = lax.ppermute(back, "col", [(0, 2), (2, 0)])
     mine, back = lax.optimization_barrier((mine, back))
     diagonal = swap(mine, "row", 6, 8).astype(F32)
     along = swap(mine, "row", 4, 8).astype(F32)
     across = swap(mine, "row", 2, 8).astype(F32)
-    grad_features = (part + got_back.astype(F32)).astype(BF16)
+    grad_features = (part + (odd.astype(F32) + even.astype(F32))).astype(BF16)
+    out = (pre * jax.nn.sigmoid(pre)).astype(BF16)
     along, grad_features = lax.optimization_barrier((along, grad_features))
     total = (mine.astype(F32) + across) + (along + diagonal)
     rest = swap(total, "row", 1, 8)

time: 38.6 us -> 38 us (0.984)
  waiting for transfers between devices: 13 us -> 9.83 us
  starting transfers between devices: 14.5 us -> 17.1 us
  other arithmetic: 1.58 us -> 2.35 us
  Pallas kernels: 4.28 us -> 3.61 us
    ppermute x12 -> x11, waiting for transfers between devices: 13 us -> 5.59 us  [swap(): return lax.ppermute(value, axis, [(i, i ^ mask) for i in range(size)])]
    ppermute x0 -> x2, waiting for transfers between devices: none -> 4.25 us  [the longest x1 4.24 us: four_by_eight(): even = lax.ppermute(back, 'col', [(0, 2), (2, 0)])]
    ppermute x0 -> x2, starting transfers between devices: none -> 2.6 us  [the longest x1 1.93 us: four_by_eight(): even = lax.ppermute(back, 'col', [(0, 2), (2, 0)])]
    convert_element_type x1 -> x2, other arithmetic: 0.68 us -> 1.44 us  [the longest x1 0.73 us: four_by_eight(): out = (pre * jax.nn.sigmoid(pre)).astype(BF16)]
    pallas_call x1, Pallas kernels: 1.13 us -> 0.46 us  [four_by_eight(): pl.pallas_call(own_kernel, out_shape=(jax.ShapeDtypeStruct((rows, width),...]
    ppermute x12 -> x11, starting transfers between devices: 14.5 us -> 14.5 us  [swap(): return lax.ppermute(value, axis, [(i, i ^ mask) for i in range(size)])]
  transfers between devices with their start and end apart: 12 -> 13, of which waited for: 6 -> 6; matrix products, arithmetic and copies ran while one was open for 2% -> 4% of each run, Pallas kernels for 8% -> 6%
where the time goes in v3:
time: 38 us; the launch traced here: 37.7 us
  starting transfers between devices  17.1 us (45%)
  waiting for transfers between devices  9.83 us (26%)
  Pallas kernels  3.61 us (10%)
  local copies, waits for them, and re-layouts  3.45 us (9%)
  other arithmetic  2.35 us (6%)
  between operations  1.44 us (4%)
    ppermute x11, starting transfers between devices, swap(): return lax.ppermute(value, axis, [(i, i ^ mask) for i in range(size)])  14.5 us
    ppermute x11, waiting for transfers between devices, swap(): return lax.ppermute(value, axis, [(i, i ^ mask) for i in range(size)])  5.59 us
    ppermute x1, waiting for transfers between devices, four_by_eight(): even = lax.ppermute(back, 'col', [(0, 2), (2, 0)])  4.24 us
    unnamed x10, local copies, waits for them, and re-layouts  3.44 us
    ppermute x1, starting transfers between devices, four_by_eight(): even = lax.ppermute(back, 'col', [(0, 2), (2, 0)])  1.93 us
    pallas_call x1, Pallas kernels, four_by_eight(): pl.pallas_call(functools.partial(pair_kernel, scale, slots), out_shape=(b...  1.24 us
  transfers between devices with their start and end apart: 13, of which 6 were waited for; matrix products, arithmetic and copies ran while one was open for 4% of the time, Pallas kernels for 6%

profile of v3, /device:TPU:0, one launch (start us, length us, event | category | flops | bytes accessed | tf_op | source)
XLA Modules:
  0.0 37.7 jit_solution(11739696796254596986)
XLA Ops:
  0.6 3.1 %collective-permute-start = (bf16[128,512]{1,0:T(8,128)(2,1)}, bf16[128,512]{1,0:T(8,128)(2,1)S(1)}, u32[]{:S(2)}, u32[]{:S(2)}) collective-permute-start(bf16[128,512]{1,0:T(8,128)(2,1)} %f.1), channel_id=1, source_target_pairs={{0,1},{1,0},{2,3},{3,2},{4,5},{5,4},{6,7},{7,6},{8,9},{9,8},{10,11... | collective-permute-start | bytes 393224 | tf_op jit(solution)/shard_map/ppermute | solution.py:86
  3.7 2.6 %collective-permute-start.1 = (bf16[128,512]{1,0:T(8,128)(2,1)}, bf16[128,512]{1,0:T(8,128)(2,1)S(1)}, u32[]{:S(2)}, u32[]{:S(2)}) collective-permute-start(bf16[128,512]{1,0:T(8,128)(2,1)} %f.1), channel_id=1, source_target_pairs={{0,2},{1,3},{2,0},{3,1},{4,6},{5,7},{6,4},{7,5},{8,10},{9,11},{10,... | collective-permute-start | bytes 393224 | tf_op jit(solution)/shard_map/ppermute | solution.py:86
  6.3 0.9 %collective-permute-start.4 = (bf16[128,512]{1,0:T(8,128)(2,1)}, bf16[128,512]{1,0:T(8,128)(2,1)S(1)}, u32[]{:S(2)}, u32[]{:S(2)}) collective-permute-start(bf16[128,512]{1,0:T(8,128)(2,1)} %ct.1), channel_id=1, source_target_pairs={{0,1},{1,0},{2,3},{3,2},{4,5},{5,4},{6,7},{7,6},{8,9},{9,8},{10,11... | collective-permute-start | bytes 393224 | tf_op jit(solution)/shard_map/ppermute | solution.py:86
  7.9 0.8 %copy-done.3 = bf16[2,128,128]{2,1,0:T(8,128)(2,1)S(1)} copy-done((bf16[2,128,128]{2,1,0:T(8,128)(2,1)S(1)}, bf16[2,128,128]{2,1,0:T(8,128)(2,1)}, u32[]{:S(2)}) %copy-start.3) | copy-done | bytes 65560
  8.7 0.7 %copy-done.4 = s32[1,2]{1,0:T(1,128)S(1)} copy-done((s32[1,2]{1,0:T(1,128)S(1)}, s32[1,2]{1,0:T(1,128)}, u32[]{:S(2)}) %copy-start.4) | copy-done | bytes 32
  9.4 0.5 %shard_map.85.tp = bf16[288,128]{1,0:T(8,128)(2,1)S(1)} custom-call(s32[1,2]{1,0:T(1,128)S(1)} %copy-done.4, s32[1]{0:T(128)S(6)} %copy.9.count, bf16[2,128,128]{2,1,0:T(8,128)(2,1)S(1)} %copy-done.3), custom_call_target="tpu_custom_call" | custom-call | tf_op jit(solution)/shard_map/pallas_call | solution.py:187
  9.9 1.2 %collective-permute-start.3 = (bf16[288,128]{1,0:T(8,128)(2,1)S(1)}, bf16[288,128]{1,0:T(8,128)(2,1)S(1)}, u32[]{:S(2)}, u32[]{:S(2)}) collective-permute-start(bf16[288,128]{1,0:T(8,128)(2,1)S(1)} %shard_map.85.tp), channel_id=1, source_target_pairs={{0,1},{1,0},{2,3},{3,2},{4,5},{5,4},{6,7},{7,6},{8,9},{9,8},{10,11... | collective-permute-start | bytes 221192 | tf_op jit(solution)/shard_map/ppermute | solution.py:86
  11.2 1.0 %copy-done = bf16[512,512]{1,0:T(8,128)(2,1)S(1)} copy-done((bf16[512,512]{1,0:T(8,128)(2,1)S(1)}, bf16[512,512]{1,0:T(8,128)(2,1)}, u32[]{:S(2)}) %copy-start) | copy-done | bytes 524312
  12.2 0.9 %copy-done.2 = bf16[128,512]{1,0:T(8,128)(2,1)S(1)} copy-done((bf16[128,512]{1,0:T(8,128)(2,1)S(1)}, bf16[128,512]{1,0:T(8,128)(2,1)}, u32[]{:S(2)}) %copy-start.2) | copy-done | bytes 131096
  13.1 0.6 %shard_map.86 = (bf16[128,512]{1,0:T(8,128)(2,1)S(1)}, bf16[128,512]{1,0:T(8,128)(2,1)S(1)}, bf16[512,512]{1,0:T(8,128)(2,1)S(1)}, bf16[128,512]{1,0:T(8,128)(2,1)S(1)}) custom-call(s32[2]{0:T(128)S(1)} %pad_add_fusion.where, bf16[288,128]{1,0:T(8,128)(2,1)S(1)} %shard_map.85.tp, bf16[128,512]{1,0:T(8,128)(2,1)S(1)} %copy-done.1, ...), custom_call_target="tpu_custom_call" | custom-call | tf_op jit(solution)/shard_map/pallas_call | solution.py:195
  13.8 3.1 %collective-permute-done.1.f2 = bf16[128,512]{1,0:T(8,128)(2,1)S(1)} collective-permute-done((bf16[128,512]{1,0:T(8,128)(2,1)}, bf16[128,512]{1,0:T(8,128)(2,1)S(1)}, u32[]{:S(2)}, u32[]{:S(2)}) %collective-permute-start.1) | collective-permute-done | bytes 131104 | tf_op jit(solution)/shard_map/ppermute | solution.py:86
  17.4 1.2 %shard_map.88 = (bf16[128,512]{1,0:T(8,128)(2,1)S(1)}, bf16[128,512]{1,0:T(8,128)(2,1)S(1)}, f32[2,64,512]{2,1,0:T(8,128)S(1)}, bf16[2,64,512]{2,1,0:T(8,128)(2,1)S(1)}) custom-call(s32[2]{0:T(128)S(1)} %pad_add_fusion.where, bf16[256,512]{1,0:T(8,128)(2,1)S(1)} %get-tuple-element.28.near, bf16[256,512]{1,0:T(8,128)(2,1)S(1)} %get-tuple-element.29.far, ...), custom_call_target="tpu_custom_call" | custom-call | flops 268435456 | bytes 2097152 | tf_op jit(solution)/shard_map/pallas_call | solution.py:220
  18.8 1.3 %collective-permute-done.5 = bf16[2,64,512]{2,1,0:T(8,128)(2,1)S(1)} collective-permute-done((bf16[2,64,512]{2,1,0:T(8,128)(2,1)S(1)}, bf16[2,64,512]{2,1,0:T(8,128)(2,1)S(1)}, u32[]{:S(2)}, u32[]{:S(2)}) %collective-permute-start.5) | collective-permute-done | bytes 131104 | tf_op jit(solution)/shard_map/ppermute | solution.py:86
  20.2 3.0 %collective-permute-start.6 = (bf16[64,512]{1,0:T(8,128)(2,1)S(1)}, bf16[64,512]{1,0:T(8,128)(2,1)S(1)}, u32[]{:S(2)}, u32[]{:S(2)}) collective-permute-start(bf16[64,512]{1,0:T(8,128)(2,1)S(1)} %fusion.2), channel_id=1, source_target_pairs={{0,2},{1,3},{2,0},{3,1},{4,6},{5,7},{6,4},{7,5},{8,10},{9,11},{10,... | collective-permute-start | bytes 196616 | tf_op jit(solution)/shard_map/ppermute | solution.py:86
  23.2 0.7 %shard_map.89 = (bf16[128,512]{1,0:T(8,128)(2,1)S(1)}, f32[128,512]{1,0:T(8,128)S(1)}) custom-call(bf16[128,512]{1,0:T(8,128)(2,1)S(1)} %get-tuple-element.31.gp0, bf16[128,512]{1,0:T(8,128)(2,1)S(1)} %get-tuple-element.36.gp1, bf16[128,512]{1,0:T(8,128)(2,1)S(1)} %get-tuple-element.24.adj.adj0, bf16[128,512]{1,0:T(8,128)(2,1)S(1)} %get-tuple-element.37.adj1, ...), custom_call_target="tpu_custom_call" | custom-call | flops 268435456 | bytes 2097152 | tf_op jit(solution)/shard_map/pallas_call | solution.py:245
  23.9 1.9 %collective-permute-start.9 = (bf16[128,512]{1,0:T(8,128)(2,1)S(1)}, bf16[128,512]{1,0:T(8,128)(2,1)S(1)}, u32[]{:S(2)}, u32[]{:S(2)}) collective-permute-start(bf16[128,512]{1,0:T(8,128)(2,1)S(1)} %get-tuple-element.38), channel_id=1, source_target_pairs={{0,2},{2,0},{4,6},{6,4},{8,10},{10,8},{12,14},{14,12},{16,18},{18,... | collective-permute-start | bytes 393224 | tf_op jit(solution)/shard_map/ppermute | solution.py:259
  25.9 0.7 %collective-permute-start.8 = (bf16[128,512]{1,0:T(8,128)(2,1)S(1)}, bf16[128,512]{1,0:T(8,128)(2,1)S(1)}, u32[]{:S(2)}, u32[]{:S(2)}) collective-permute-start(bf16[128,512]{1,0:T(8,128)(2,1)S(1)} %get-tuple-element.38), channel_id=1, source_target_pairs={{1,3},{3,1},{5,7},{7,5},{9,11},{11,9},{13,15},{15,13},{17,19},{19,... | collective-permute-start | bytes 393224 | tf_op jit(solution)/shard_map/ppermute | solution.py:258
  27.0 1.6 %collective-permute-start.7 = (bf16[64,512]{1,0:T(8,128)(2,1)S(1)}, bf16[64,512]{1,0:T(8,128)(2,1)S(1)}, u32[]{:S(2)}, u32[]{:S(2)}) collective-permute-start(bf16[64,512]{1,0:T(8,128)(2,1)S(1)} %fusion.1), channel_id=1, source_target_pairs={{0,16},{4,20},{8,24},{12,28},{16,0},{20,4},{24,8},{28,12},{1,17},{... | collective-permute-start | bytes 196616 | tf_op jit(solution)/shard_map/ppermute | solution.py:86
  28.6 1.4 %collective-permute-start.11 = (bf16[64,512]{1,0:T(8,128)(2,1)S(1)}, bf16[64,512]{1,0:T(8,128)(2,1)S(1)}, u32[]{:S(2)}, u32[]{:S(2)}) collective-permute-start(bf16[64,512]{1,0:T(8,128)(2,1)S(1)} %fusion.1), channel_id=1, source_target_pairs={{0,24},{4,28},{8,16},{12,20},{16,8},{20,12},{24,0},{28,4},{1,25},{... | collective-permute-start | bytes 196616 | tf_op jit(solution)/shard_map/ppermute | solution.py:86
  30.5 4.2 %collective-permute-done.9 = bf16[128,512]{1,0:T(8,128)(2,1)S(1)} collective-permute-done((bf16[128,512]{1,0:T(8,128)(2,1)S(1)}, bf16[128,512]{1,0:T(8,128)(2,1)S(1)}, u32[]{:S(2)}, u32[]{:S(2)}) %collective-permute-start.9) | collective-permute-done | bytes 131104 | tf_op jit(solution)/shard_map/ppermute | solution.py:259
  34.8 0.7 %add_convert_fusion = bf16[128,512]{1,0:T(8,128)(2,1)} fusion(f32[128,512]{1,0:T(8,128)S(1)} %get-tuple-element.40, bf16[128,512]{1,0:T(8,128)(2,1)S(1)} %collective-permute-done.9, bf16[128,512]{1,0:T(8,128)(2,1)S(1)} %collective-permute-done.8), kind=kLoop, calls=%fused_computation.1 | loop fusion | flops 327680 | bytes 655360 | tf_op jit(solution)/shard_map/convert_element_type | solution.py:264
  35.7 0.7 %multiply_convert_fusion = bf16[128,512]{1,0:T(8,128)(2,1)} fusion(f32[128,512]{1,0:T(8,128)S(1)} %get-tuple-element.27), kind=kLoop, calls=%fused_computation.3 | loop fusion | flops 327680 | bytes 393216 | tf_op jit(solution)/shard_map/convert_element_type | solution.py:265
  36.4 0.6 %collective-permute-done.12 = f32[64,512]{1,0:T(8,128)S(1)} collective-permute-done((f32[64,512]{1,0:T(8,128)S(1)}, f32[64,512]{1,0:T(8,128)S(1)}, u32[]{:S(2)}, u32[]{:S(2)}) %collective-permute-start.12) | collective-permute-done | bytes 131104 | tf_op jit(solution)/shard_map/ppermute | solution.py:86
  37.0 0.7 %pad_maximum_fusion = f32[128,512]{1,0:T(8,128)} fusion(f32[64,512]{1,0:T(8,128)S(1)} %get-tuple-element.44, f32[64,512]{1,0:T(8,128)S(1)} %get-tuple-element.43), kind=kLoop, calls=%fused_computation | loop fusion | flops 65536 | bytes 524288 | tf_op jit(solution)/shard_map/concatenate | solution.py:271
  (27 shorter events, 1.9 us)
Async XLA Ops:
  0.6 10.6 %copy-start.1 = (bf16[128,512]{1,0:T(8,128)(2,1)S(1)}, bf16[128,512]{1,0:T(8,128)(2,1)}, u32[]{:S(2)}) copy-start(bf16[128,512]{1,0:T(8,128)(2,1)} %f.1) | copy-start | bytes 393220
  0.6 13.1 %collective-permute-start = (bf16[128,512]{1,0:T(8,128)(2,1)}, bf16[128,512]{1,0:T(8,128)(2,1)S(1)}, u32[]{:S(2)}, u32[]{:S(2)}) collective-permute-start(bf16[128,512]{1,0:T(8,128)(2,1)} %f.1), channel_id=1, source_target_pairs={{0,1},{1,0},{2,3},{3,2},{4,5},{5,4},{6,7},{7,6},{8,9},{9,8},{10,11... | collective-permute-start | bytes 393224 | tf_op jit(solution)/shard_map/ppermute | solution.py:86
  3.7 13.2 %collective-permute-start.1 = (bf16[128,512]{1,0:T(8,128)(2,1)}, bf16[128,512]{1,0:T(8,128)(2,1)S(1)}, u32[]{:S(2)}, u32[]{:S(2)}) collective-permute-start(bf16[128,512]{1,0:T(8,128)(2,1)} %f.1), channel_id=1, source_target_pairs={{0,2},{1,3},{2,0},{3,1},{4,6},{5,7},{6,4},{7,5},{8,10},{9,11},{10,... | collective-permute-start | bytes 393224 | tf_op jit(solution)/shard_map/ppermute | solution.py:86
  6.3 10.6 %collective-permute-start.2 = (bf16[128,512]{1,0:T(8,128)(2,1)}, bf16[128,512]{1,0:T(8,128)(2,1)S(1)}, u32[]{:S(2)}, u32[]{:S(2)}) collective-permute-start(bf16[128,512]{1,0:T(8,128)(2,1)} %f.1), channel_id=1, source_target_pairs={{0,3},{1,2},{2,1},{3,0},{4,7},{5,6},{6,5},{7,4},{8,11},{9,10},{10,... | collective-permute-start | bytes 393224 | tf_op jit(solution)/shard_map/ppermute | solution.py:86
  6.3 11.1 %collective-permute-start.4 = (bf16[128,512]{1,0:T(8,128)(2,1)}, bf16[128,512]{1,0:T(8,128)(2,1)S(1)}, u32[]{:S(2)}, u32[]{:S(2)}) collective-permute-start(bf16[128,512]{1,0:T(8,128)(2,1)} %ct.1), channel_id=1, source_target_pairs={{0,1},{1,0},{2,3},{3,2},{4,5},{5,4},{6,7},{7,6},{8,9},{9,8},{10,11... | collective-permute-start | bytes 393224 | tf_op jit(solution)/shard_map/ppermute | solution.py:86
  7.9 0.8 %copy-start.3 = (bf16[2,128,128]{2,1,0:T(8,128)(2,1)S(1)}, bf16[2,128,128]{2,1,0:T(8,128)(2,1)}, u32[]{:S(2)}) copy-start(bf16[2,128,128]{2,1,0:T(8,128)(2,1)} %blocks.1) | copy-start | bytes 196612
  8.7 0.7 %copy-start.4 = (s32[1,2]{1,0:T(1,128)S(1)}, s32[1,2]{1,0:T(1,128)}, u32[]{:S(2)}) copy-start(s32[1,2]{1,0:T(1,128)} %index.1) | copy-start | bytes 28
  9.9 7.5 %collective-permute-start.3 = (bf16[288,128]{1,0:T(8,128)(2,1)S(1)}, bf16[288,128]{1,0:T(8,128)(2,1)S(1)}, u32[]{:S(2)}, u32[]{:S(2)}) collective-permute-start(bf16[288,128]{1,0:T(8,128)(2,1)S(1)} %shard_map.85.tp), channel_id=1, source_target_pairs={{0,1},{1,0},{2,3},{3,2},{4,5},{5,4},{6,7},{7,6},{8,9},{9,8},{10,11... | collective-permute-start | bytes 221192 | tf_op jit(solution)/shard_map/ppermute | solution.py:86
  11.2 1.0 %copy-start = (bf16[512,512]{1,0:T(8,128)(2,1)S(1)}, bf16[512,512]{1,0:T(8,128)(2,1)}, u32[]{:S(2)}) copy-start(bf16[512,512]{1,0:T(8,128)(2,1)} %w.1) | copy-start | bytes 1572868
  12.2 0.9 %copy-start.2 = (bf16[128,512]{1,0:T(8,128)(2,1)S(1)}, bf16[128,512]{1,0:T(8,128)(2,1)}, u32[]{:S(2)}) copy-start(bf16[128,512]{1,0:T(8,128)(2,1)} %ct.1) | copy-start | bytes 393220
  18.7 1.4 %collective-permute-start.5 = (bf16[2,64,512]{2,1,0:T(8,128)(2,1)S(1)}, bf16[2,64,512]{2,1,0:T(8,128)(2,1)S(1)}, u32[]{:S(2)}, u32[]{:S(2)}) collective-permute-start(bf16[2,64,512]{2,1,0:T(8,128)(2,1)S(1)} %get-tuple-element.33), channel_id=1, source_target_pairs={{0,4},{4,0},{8,12},{12,8},{16,20},{20,16},{24,28},{28,24},{1,5},{5... | collective-permute-start | bytes 393224 | tf_op jit(solution)/shard_map/ppermute | solution.py:86
  20.2 6.8 %collective-permute-start.6 = (bf16[64,512]{1,0:T(8,128)(2,1)S(1)}, bf16[64,512]{1,0:T(8,128)(2,1)S(1)}, u32[]{:S(2)}, u32[]{:S(2)}) collective-permute-start(bf16[64,512]{1,0:T(8,128)(2,1)S(1)} %fusion.2), channel_id=1, source_target_pairs={{0,2},{1,3},{2,0},{3,1},{4,6},{5,7},{6,4},{7,5},{8,10},{9,11},{10,... | collective-permute-start | bytes 196616 | tf_op jit(solution)/shard_map/ppermute | solution.py:86
  23.9 10.9 %collective-permute-start.9 = (bf16[128,512]{1,0:T(8,128)(2,1)S(1)}, bf16[128,512]{1,0:T(8,128)(2,1)S(1)}, u32[]{:S(2)}, u32[]{:S(2)}) collective-permute-start(bf16[128,512]{1,0:T(8,128)(2,1)S(1)} %get-tuple-element.38), channel_id=1, source_target_pairs={{0,2},{2,0},{4,6},{6,4},{8,10},{10,8},{12,14},{14,12},{16,18},{18,... | collective-permute-start | bytes 393224 | tf_op jit(solution)/shard_map/ppermute | solution.py:259
  25.9 8.9 %collective-permute-start.8 = (bf16[128,512]{1,0:T(8,128)(2,1)S(1)}, bf16[128,512]{1,0:T(8,128)(2,1)S(1)}, u32[]{:S(2)}, u32[]{:S(2)}) collective-permute-start(bf16[128,512]{1,0:T(8,128)(2,1)S(1)} %get-tuple-element.38), channel_id=1, source_target_pairs={{1,3},{3,1},{5,7},{7,5},{9,11},{11,9},{13,15},{15,13},{17,19},{19,... | collective-permute-start | bytes 393224 | tf_op jit(solution)/shard_map/ppermute | solution.py:258
  27.0 8.5 %collective-permute-start.7 = (bf16[64,512]{1,0:T(8,128)(2,1)S(1)}, bf16[64,512]{1,0:T(8,128)(2,1)S(1)}, u32[]{:S(2)}, u32[]{:S(2)}) collective-permute-start(bf16[64,512]{1,0:T(8,128)(2,1)S(1)} %fusion.1), channel_id=1, source_target_pairs={{0,16},{4,20},{8,24},{12,28},{16,0},{20,4},{24,8},{28,12},{1,17},{... | collective-permute-start | bytes 196616 | tf_op jit(solution)/shard_map/ppermute | solution.py:86
  28.6 6.9 %collective-permute-start.11 = (bf16[64,512]{1,0:T(8,128)(2,1)S(1)}, bf16[64,512]{1,0:T(8,128)(2,1)S(1)}, u32[]{:S(2)}, u32[]{:S(2)}) collective-permute-start(bf16[64,512]{1,0:T(8,128)(2,1)S(1)} %fusion.1), channel_id=1, source_target_pairs={{0,24},{4,28},{8,16},{12,20},{16,8},{20,12},{24,0},{28,4},{1,25},{... | collective-permute-start | bytes 196616 | tf_op jit(solution)/shard_map/ppermute | solution.py:86
  30.0 5.5 %collective-permute-start.10 = (bf16[64,512]{1,0:T(8,128)(2,1)S(1)}, bf16[64,512]{1,0:T(8,128)(2,1)S(1)}, u32[]{:S(2)}, u32[]{:S(2)}) collective-permute-start(bf16[64,512]{1,0:T(8,128)(2,1)S(1)} %fusion.1), channel_id=1, source_target_pairs={{0,8},{4,12},{8,0},{12,4},{16,24},{20,28},{24,16},{28,20},{1,9},{5... | collective-permute-start | bytes 196616 | tf_op jit(solution)/shard_map/ppermute | solution.py:86
  35.6 1.4 %collective-permute-start.12 = (f32[64,512]{1,0:T(8,128)S(1)}, f32[64,512]{1,0:T(8,128)S(1)}, u32[]{:S(2)}, u32[]{:S(2)}) collective-permute-start(f32[64,512]{1,0:T(8,128)S(1)} %add_add_fusion), channel_id=1, source_target_pairs={{0,4},{4,0},{8,12},{12,8},{16,20},{20,16},{24,28},{28,24},{1,5},{5... | collective-permute-start | bytes 393224 | tf_op jit(solution)/shard_map/ppermute | solution.py:86

commit v4 on v3

--- a/solution.py
+++ b/solution.py
@@ -261,11 +261,11 @@
     diagonal = swap(mine, "row", 6, 8).astype(F32)
     along = swap(mine, "row", 4, 8).astype(F32)
     across = swap(mine, "row", 2, 8).astype(F32)
-    grad_features = (part + (odd.astype(F32) + even.astype(F32))).astype(BF16)
+    along, even, odd = lax.optimization_barrier((along, even, odd))
     out = (pre * jax.nn.sigmoid(pre)).astype(BF16)
-    along, grad_features = lax.optimization_barrier((along, grad_features))
     total = (mine.astype(F32) + across) + (along + diagonal)
     rest = swap(total, "row", 1, 8)
+    grad_features = (part + (odd.astype(F32) + even.astype(F32))).astype(BF16)
     first = jnp.where(half == 0, total, rest)
     second = jnp.where(half == 0, rest, total)
     grad_weight = jnp.concatenate([first, second], axis=0)

time: 38 us -> 37.3 us (0.982)
  waiting for transfers between devices: 9.83 us -> 9.11 us
    ppermute x1, waiting for transfers between devices: 4.24 us -> 3.44 us  [four_by_eight(): even = lax.ppermute(back, 'col', [(0, 2), (2, 0)])]
  transfers between devices with their start and end apart: 13 -> 13, of which waited for: 6 -> 7; matrix products, arithmetic and copies ran while one was open for 4% -> 4% of each run, Pallas kernels for 6% -> 6%
where the time goes in v4:
time: 37.3 us; the launch traced here: 37 us
  starting transfers between devices  17.1 us (46%)
  waiting for transfers between devices  9.11 us (24%)
  Pallas kernels  3.61 us (10%)
  local copies, waits for them, and re-layouts  3.45 us (9%)
  other arithmetic  2.35 us (6%)
  between operations  1.42 us (4%)
    ppermute x11, starting transfers between devices, swap(): return lax.ppermute(value, axis, [(i, i ^ mask) for i in range(size)])  14.5 us
    ppermute x11, waiting for transfers between devices, swap(): return lax.ppermute(value, axis, [(i, i ^ mask) for i in range(size)])  5.66 us
    ppermute x1, waiting for transfers between devices, four_by_eight(): even = lax.ppermute(back, 'col', [(0, 2), (2, 0)])  3.44 us
    unnamed x10, local copies, waits for them, and re-layouts  3.44 us
    ppermute x1, starting transfers between devices, four_by_eight(): even = lax.ppermute(back, 'col', [(0, 2), (2, 0)])  1.93 us
    pallas_call x1, Pallas kernels, four_by_eight(): pl.pallas_call(functools.partial(pair_kernel, scale, slots), out_shape=(b...  1.24 us
    pallas_call x1, Pallas kernels, four_by_eight(): pl.pallas_call(backward_kernel, out_shape=(jax.ShapeDtypeStruct((rows, wi...  0.75 us
  transfers between devices with their start and end apart: 13, of which 7 were waited for; matrix products, arithmetic and copies ran while one was open for 4% of the time, Pallas kernels for 6%

profile of v4, /device:TPU:0, one launch (start us, length us, event | category | flops | bytes accessed | tf_op | source)
XLA Modules:
  0.0 37.0 jit_solution(13422775987786233176)
XLA Ops:
  0.6 3.1 %collective-permute-start = (bf16[128,512]{1,0:T(8,128)(2,1)}, bf16[128,512]{1,0:T(8,128)(2,1)S(1)}, u32[]{:S(2)}, u32[]{:S(2)}) collective-permute-start(bf16[128,512]{1,0:T(8,128)(2,1)} %f.1), channel_id=1, source_target_pairs={{0,1},{1,0},{2,3},{3,2},{4,5},{5,4},{6,7},{7,6},{8,9},{9,8},{10,11... | collective-permute-start | bytes 393224 | tf_op jit(solution)/shard_map/ppermute | solution.py:86
  3.7 2.6 %collective-permute-start.1 = (bf16[128,512]{1,0:T(8,128)(2,1)}, bf16[128,512]{1,0:T(8,128)(2,1)S(1)}, u32[]{:S(2)}, u32[]{:S(2)}) collective-permute-start(bf16[128,512]{1,0:T(8,128)(2,1)} %f.1), channel_id=1, source_target_pairs={{0,2},{1,3},{2,0},{3,1},{4,6},{5,7},{6,4},{7,5},{8,10},{9,11},{10,... | collective-permute-start | bytes 393224 | tf_op jit(solution)/shard_map/ppermute | solution.py:86
  6.3 0.9 %collective-permute-start.4 = (bf16[128,512]{1,0:T(8,128)(2,1)}, bf16[128,512]{1,0:T(8,128)(2,1)S(1)}, u32[]{:S(2)}, u32[]{:S(2)}) collective-permute-start(bf16[128,512]{1,0:T(8,128)(2,1)} %ct.1), channel_id=1, source_target_pairs={{0,1},{1,0},{2,3},{3,2},{4,5},{5,4},{6,7},{7,6},{8,9},{9,8},{10,11... | collective-permute-start | bytes 393224 | tf_op jit(solution)/shard_map/ppermute | solution.py:86
  7.9 0.8 %copy-done.3 = bf16[2,128,128]{2,1,0:T(8,128)(2,1)S(1)} copy-done((bf16[2,128,128]{2,1,0:T(8,128)(2,1)S(1)}, bf16[2,128,128]{2,1,0:T(8,128)(2,1)}, u32[]{:S(2)}) %copy-start.3) | copy-done | bytes 65560
  8.7 0.7 %copy-done.4 = s32[1,2]{1,0:T(1,128)S(1)} copy-done((s32[1,2]{1,0:T(1,128)S(1)}, s32[1,2]{1,0:T(1,128)}, u32[]{:S(2)}) %copy-start.4) | copy-done | bytes 32
  9.4 0.5 %shard_map.85.tp = bf16[288,128]{1,0:T(8,128)(2,1)S(1)} custom-call(s32[1,2]{1,0:T(1,128)S(1)} %copy-done.4, s32[1]{0:T(128)S(6)} %copy.9.count, bf16[2,128,128]{2,1,0:T(8,128)(2,1)S(1)} %copy-done.3), custom_call_target="tpu_custom_call" | custom-call | tf_op jit(solution)/shard_map/pallas_call | solution.py:187
  9.9 1.2 %collective-permute-start.3 = (bf16[288,128]{1,0:T(8,128)(2,1)S(1)}, bf16[288,128]{1,0:T(8,128)(2,1)S(1)}, u32[]{:S(2)}, u32[]{:S(2)}) collective-permute-start(bf16[288,128]{1,0:T(8,128)(2,1)S(1)} %shard_map.85.tp), channel_id=1, source_target_pairs={{0,1},{1,0},{2,3},{3,2},{4,5},{5,4},{6,7},{7,6},{8,9},{9,8},{10,11... | collective-permute-start | bytes 221192 | tf_op jit(solution)/shard_map/ppermute | solution.py:86
  11.2 1.0 %copy-done = bf16[512,512]{1,0:T(8,128)(2,1)S(1)} copy-done((bf16[512,512]{1,0:T(8,128)(2,1)S(1)}, bf16[512,512]{1,0:T(8,128)(2,1)}, u32[]{:S(2)}) %copy-start) | copy-done | bytes 524312
  12.2 0.9 %copy-done.2 = bf16[128,512]{1,0:T(8,128)(2,1)S(1)} copy-done((bf16[128,512]{1,0:T(8,128)(2,1)S(1)}, bf16[128,512]{1,0:T(8,128)(2,1)}, u32[]{:S(2)}) %copy-start.2) | copy-done | bytes 131096
  13.1 0.6 %shard_map.86 = (bf16[128,512]{1,0:T(8,128)(2,1)S(1)}, bf16[128,512]{1,0:T(8,128)(2,1)S(1)}, bf16[512,512]{1,0:T(8,128)(2,1)S(1)}, bf16[128,512]{1,0:T(8,128)(2,1)S(1)}) custom-call(s32[2]{0:T(128)S(1)} %pad_add_fusion.where, bf16[288,128]{1,0:T(8,128)(2,1)S(1)} %shard_map.85.tp, bf16[128,512]{1,0:T(8,128)(2,1)S(1)} %copy-done.1, ...), custom_call_target="tpu_custom_call" | custom-call | tf_op jit(solution)/shard_map/pallas_call | solution.py:195
  13.8 3.1 %collective-permute-done.1.f2 = bf16[128,512]{1,0:T(8,128)(2,1)S(1)} collective-permute-done((bf16[128,512]{1,0:T(8,128)(2,1)}, bf16[128,512]{1,0:T(8,128)(2,1)S(1)}, u32[]{:S(2)}, u32[]{:S(2)}) %collective-permute-start.1) | collective-permute-done | bytes 131104 | tf_op jit(solution)/shard_map/ppermute | solution.py:86
  17.4 1.2 %shard_map.88 = (bf16[128,512]{1,0:T(8,128)(2,1)S(1)}, bf16[128,512]{1,0:T(8,128)(2,1)S(1)}, f32[2,64,512]{2,1,0:T(8,128)S(1)}, bf16[2,64,512]{2,1,0:T(8,128)(2,1)S(1)}) custom-call(s32[2]{0:T(128)S(1)} %pad_add_fusion.where, bf16[256,512]{1,0:T(8,128)(2,1)S(1)} %get-tuple-element.30.near, bf16[256,512]{1,0:T(8,128)(2,1)S(1)} %get-tuple-element.31.far, ...), custom_call_target="tpu_custom_call" | custom-call | flops 268435456 | bytes 2097152 | tf_op jit(solution)/shard_map/pallas_call | solution.py:220
  18.8 1.3 %collective-permute-done.5 = bf16[2,64,512]{2,1,0:T(8,128)(2,1)S(1)} collective-permute-done((bf16[2,64,512]{2,1,0:T(8,128)(2,1)S(1)}, bf16[2,64,512]{2,1,0:T(8,128)(2,1)S(1)}, u32[]{:S(2)}, u32[]{:S(2)}) %collective-permute-start.5) | collective-permute-done | bytes 131104 | tf_op jit(solution)/shard_map/ppermute | solution.py:86
  20.2 3.0 %collective-permute-start.6 = (bf16[64,512]{1,0:T(8,128)(2,1)S(1)}, bf16[64,512]{1,0:T(8,128)(2,1)S(1)}, u32[]{:S(2)}, u32[]{:S(2)}) collective-permute-start(bf16[64,512]{1,0:T(8,128)(2,1)S(1)} %fusion.2), channel_id=1, source_target_pairs={{0,2},{1,3},{2,0},{3,1},{4,6},{5,7},{6,4},{7,5},{8,10},{9,11},{10,... | collective-permute-start | bytes 196616 | tf_op jit(solution)/shard_map/ppermute | solution.py:86
  23.2 0.7 %shard_map.89 = (bf16[128,512]{1,0:T(8,128)(2,1)S(1)}, f32[128,512]{1,0:T(8,128)S(1)}) custom-call(bf16[128,512]{1,0:T(8,128)(2,1)S(1)} %get-tuple-element.29.gp0, bf16[128,512]{1,0:T(8,128)(2,1)S(1)} %get-tuple-element.36.gp1, bf16[128,512]{1,0:T(8,128)(2,1)S(1)} %get-tuple-element.25.adj.adj0, bf16[128,512]{1,0:T(8,128)(2,1)S(1)} %get-tuple-element.37.adj1, ...), custom_call_target="tpu_custom_call" | custom-call | flops 268435456 | bytes 2097152 | tf_op jit(solution)/shard_map/pallas_call | solution.py:245
  23.9 1.9 %collective-permute-start.8 = (bf16[128,512]{1,0:T(8,128)(2,1)S(1)}, bf16[128,512]{1,0:T(8,128)(2,1)S(1)}, u32[]{:S(2)}, u32[]{:S(2)}) collective-permute-start(bf16[128,512]{1,0:T(8,128)(2,1)S(1)} %get-tuple-element.40), channel_id=1, source_target_pairs={{0,2},{2,0},{4,6},{6,4},{8,10},{10,8},{12,14},{14,12},{16,18},{18,... | collective-permute-start | bytes 393224 | tf_op jit(solution)/shard_map/ppermute | solution.py:259
  25.9 0.7 %collective-permute-start.9 = (bf16[128,512]{1,0:T(8,128)(2,1)S(1)}, bf16[128,512]{1,0:T(8,128)(2,1)S(1)}, u32[]{:S(2)}, u32[]{:S(2)}) collective-permute-start(bf16[128,512]{1,0:T(8,128)(2,1)S(1)} %get-tuple-element.40), channel_id=1, source_target_pairs={{1,3},{3,1},{5,7},{7,5},{9,11},{11,9},{13,15},{15,13},{17,19},{19,... | collective-permute-start | bytes 393224 | tf_op jit(solution)/shard_map/ppermute | solution.py:258
  27.0 1.6 %collective-permute-start.7 = (bf16[64,512]{1,0:T(8,128)(2,1)S(1)}, bf16[64,512]{1,0:T(8,128)(2,1)S(1)}, u32[]{:S(2)}, u32[]{:S(2)}) collective-permute-start(bf16[64,512]{1,0:T(8,128)(2,1)S(1)} %fusion.1), channel_id=1, source_target_pairs={{0,16},{4,20},{8,24},{12,28},{16,0},{20,4},{24,8},{28,12},{1,17},{... | collective-permute-start | bytes 196616 | tf_op jit(solution)/shard_map/ppermute | solution.py:86
  28.6 1.4 %collective-permute-start.11 = (bf16[64,512]{1,0:T(8,128)(2,1)S(1)}, bf16[64,512]{1,0:T(8,128)(2,1)S(1)}, u32[]{:S(2)}, u32[]{:S(2)}) collective-permute-start(bf16[64,512]{1,0:T(8,128)(2,1)S(1)} %fusion.1), channel_id=1, source_target_pairs={{0,24},{4,28},{8,16},{12,20},{16,8},{20,12},{24,0},{28,4},{1,25},{... | collective-permute-start | bytes 196616 | tf_op jit(solution)/shard_map/ppermute | solution.py:86
  30.5 0.7 %multiply_convert_fusion = bf16[128,512]{1,0:T(8,128)(2,1)} fusion(f32[128,512]{1,0:T(8,128)S(1)} %get-tuple-element.28), kind=kLoop, calls=%fused_computation.3 | loop fusion | flops 327680 | bytes 393216 | tf_op jit(solution)/shard_map/convert_element_type | solution.py:265
  31.3 3.4 %collective-permute-done.8 = bf16[128,512]{1,0:T(8,128)(2,1)S(1)} collective-permute-done((bf16[128,512]{1,0:T(8,128)(2,1)S(1)}, bf16[128,512]{1,0:T(8,128)(2,1)S(1)}, u32[]{:S(2)}, u32[]{:S(2)}) %collective-permute-start.8) | collective-permute-done | bytes 131104 | tf_op jit(solution)/shard_map/ppermute | solution.py:259
  34.9 0.7 %add_convert_fusion = bf16[128,512]{1,0:T(8,128)(2,1)} fusion(f32[128,512]{1,0:T(8,128)S(1)} %get-tuple-element.38, bf16[128,512]{1,0:T(8,128)(2,1)S(1)} %collective-permute-done.8, bf16[128,512]{1,0:T(8,128)(2,1)S(1)} %collective-permute-done.9), kind=kLoop, calls=%fused_computation.1 | loop fusion | flops 327680 | bytes 655360 | tf_op jit(solution)/shard_map/convert_element_type | solution.py:268
  35.6 0.6 %collective-permute-done.12 = f32[64,512]{1,0:T(8,128)S(1)} collective-permute-done((f32[64,512]{1,0:T(8,128)S(1)}, f32[64,512]{1,0:T(8,128)S(1)}, u32[]{:S(2)}, u32[]{:S(2)}) %collective-permute-start.12) | collective-permute-done | bytes 131104 | tf_op jit(solution)/shard_map/ppermute | solution.py:86
  36.3 0.7 %pad_maximum_fusion = f32[128,512]{1,0:T(8,128)} fusion(f32[64,512]{1,0:T(8,128)S(1)} %get-tuple-element.46, f32[64,512]{1,0:T(8,128)S(1)} %get-tuple-element.45), kind=kLoop, calls=%fused_computation | loop fusion | flops 65536 | bytes 524288 | tf_op jit(solution)/shard_map/concatenate | solution.py:271
  (27 shorter events, 1.9 us)
Async XLA Ops:
  0.6 10.6 %copy-start.1 = (bf16[128,512]{1,0:T(8,128)(2,1)S(1)}, bf16[128,512]{1,0:T(8,128)(2,1)}, u32[]{:S(2)}) copy-start(bf16[128,512]{1,0:T(8,128)(2,1)} %f.1) | copy-start | bytes 393220
  0.6 13.1 %collective-permute-start = (bf16[128,512]{1,0:T(8,128)(2,1)}, bf16[128,512]{1,0:T(8,128)(2,1)S(1)}, u32[]{:S(2)}, u32[]{:S(2)}) collective-permute-start(bf16[128,512]{1,0:T(8,128)(2,1)} %f.1), channel_id=1, source_target_pairs={{0,1},{1,0},{2,3},{3,2},{4,5},{5,4},{6,7},{7,6},{8,9},{9,8},{10,11... | collective-permute-start | bytes 393224 | tf_op jit(solution)/shard_map/ppermute | solution.py:86
  3.7 13.2 %collective-permute-start.1 = (bf16[128,512]{1,0:T(8,128)(2,1)}, bf16[128,512]{1,0:T(8,128)(2,1)S(1)}, u32[]{:S(2)}, u32[]{:S(2)}) collective-permute-start(bf16[128,512]{1,0:T(8,128)(2,1)} %f.1), channel_id=1, source_target_pairs={{0,2},{1,3},{2,0},{3,1},{4,6},{5,7},{6,4},{7,5},{8,10},{9,11},{10,... | collective-permute-start | bytes 393224 | tf_op jit(solution)/shard_map/ppermute | solution.py:86
  6.3 10.6 %collective-permute-start.2 = (bf16[128,512]{1,0:T(8,128)(2,1)}, bf16[128,512]{1,0:T(8,128)(2,1)S(1)}, u32[]{:S(2)}, u32[]{:S(2)}) collective-permute-start(bf16[128,512]{1,0:T(8,128)(2,1)} %f.1), channel_id=1, source_target_pairs={{0,3},{1,2},{2,1},{3,0},{4,7},{5,6},{6,5},{7,4},{8,11},{9,10},{10,... | collective-permute-start | bytes 393224 | tf_op jit(solution)/shard_map/ppermute | solution.py:86
  6.3 11.1 %collective-permute-start.4 = (bf16[128,512]{1,0:T(8,128)(2,1)}, bf16[128,512]{1,0:T(8,128)(2,1)S(1)}, u32[]{:S(2)}, u32[]{:S(2)}) collective-permute-start(bf16[128,512]{1,0:T(8,128)(2,1)} %ct.1), channel_id=1, source_target_pairs={{0,1},{1,0},{2,3},{3,2},{4,5},{5,4},{6,7},{7,6},{8,9},{9,8},{10,11... | collective-permute-start | bytes 393224 | tf_op jit(solution)/shard_map/ppermute | solution.py:86
  7.9 0.8 %copy-start.3 = (bf16[2,128,128]{2,1,0:T(8,128)(2,1)S(1)}, bf16[2,128,128]{2,1,0:T(8,128)(2,1)}, u32[]{:S(2)}) copy-start(bf16[2,128,128]{2,1,0:T(8,128)(2,1)} %blocks.1) | copy-start | bytes 196612
  8.7 0.7 %copy-start.4 = (s32[1,2]{1,0:T(1,128)S(1)}, s32[1,2]{1,0:T(1,128)}, u32[]{:S(2)}) copy-start(s32[1,2]{1,0:T(1,128)} %index.1) | copy-start | bytes 28
  9.9 7.5 %collective-permute-start.3 = (bf16[288,128]{1,0:T(8,128)(2,1)S(1)}, bf16[288,128]{1,0:T(8,128)(2,1)S(1)}, u32[]{:S(2)}, u32[]{:S(2)}) collective-permute-start(bf16[288,128]{1,0:T(8,128)(2,1)S(1)} %shard_map.85.tp), channel_id=1, source_target_pairs={{0,1},{1,0},{2,3},{3,2},{4,5},{5,4},{6,7},{7,6},{8,9},{9,8},{10,11... | collective-permute-start | bytes 221192 | tf_op jit(solution)/shard_map/ppermute | solution.py:86
  11.2 1.0 %copy-start = (bf16[512,512]{1,0:T(8,128)(2,1)S(1)}, bf16[512,512]{1,0:T(8,128)(2,1)}, u32[]{:S(2)}) copy-start(bf16[512,512]{1,0:T(8,128)(2,1)} %w.1) | copy-start | bytes 1572868
  12.2 0.9 %copy-start.2 = (bf16[128,512]{1,0:T(8,128)(2,1)S(1)}, bf16[128,512]{1,0:T(8,128)(2,1)}, u32[]{:S(2)}) copy-start(bf16[128,512]{1,0:T(8,128)(2,1)} %ct.1) | copy-start | bytes 393220
  18.7 1.4 %collective-permute-start.5 = (bf16[2,64,512]{2,1,0:T(8,128)(2,1)S(1)}, bf16[2,64,512]{2,1,0:T(8,128)(2,1)S(1)}, u32[]{:S(2)}, u32[]{:S(2)}) collective-permute-start(bf16[2,64,512]{2,1,0:T(8,128)(2,1)S(1)} %get-tuple-element.34), channel_id=1, source_target_pairs={{0,4},{4,0},{8,12},{12,8},{16,20},{20,16},{24,28},{28,24},{1,5},{5... | collective-permute-start | bytes 393224 | tf_op jit(solution)/shard_map/ppermute | solution.py:86
  20.2 6.8 %collective-permute-start.6 = (bf16[64,512]{1,0:T(8,128)(2,1)S(1)}, bf16[64,512]{1,0:T(8,128)(2,1)S(1)}, u32[]{:S(2)}, u32[]{:S(2)}) collective-permute-start(bf16[64,512]{1,0:T(8,128)(2,1)S(1)} %fusion.2), channel_id=1, source_target_pairs={{0,2},{1,3},{2,0},{3,1},{4,6},{5,7},{6,4},{7,5},{8,10},{9,11},{10,... | collective-permute-start | bytes 196616 | tf_op jit(solution)/shard_map/ppermute | solution.py:86
  23.9 10.9 %collective-permute-start.8 = (bf16[128,512]{1,0:T(8,128)(2,1)S(1)}, bf16[128,512]{1,0:T(8,128)(2,1)S(1)}, u32[]{:S(2)}, u32[]{:S(2)}) collective-permute-start(bf16[128,512]{1,0:T(8,128)(2,1)S(1)} %get-tuple-element.40), channel_id=1, source_target_pairs={{0,2},{2,0},{4,6},{6,4},{8,10},{10,8},{12,14},{14,12},{16,18},{18,... | collective-permute-start | bytes 393224 | tf_op jit(solution)/shard_map/ppermute | solution.py:259
  25.9 8.9 %collective-permute-start.9 = (bf16[128,512]{1,0:T(8,128)(2,1)S(1)}, bf16[128,512]{1,0:T(8,128)(2,1)S(1)}, u32[]{:S(2)}, u32[]{:S(2)}) collective-permute-start(bf16[128,512]{1,0:T(8,128)(2,1)S(1)} %get-tuple-element.40), channel_id=1, source_target_pairs={{1,3},{3,1},{5,7},{7,5},{9,11},{11,9},{13,15},{15,13},{17,19},{19,... | collective-permute-start | bytes 393224 | tf_op jit(solution)/shard_map/ppermute | solution.py:258
  27.0 4.3 %collective-permute-start.7 = (bf16[64,512]{1,0:T(8,128)(2,1)S(1)}, bf16[64,512]{1,0:T(8,128)(2,1)S(1)}, u32[]{:S(2)}, u32[]{:S(2)}) collective-permute-start(bf16[64,512]{1,0:T(8,128)(2,1)S(1)} %fusion.1), channel_id=1, source_target_pairs={{0,16},{4,20},{8,24},{12,28},{16,0},{20,4},{24,8},{28,12},{1,17},{... | collective-permute-start | bytes 196616 | tf_op jit(solution)/shard_map/ppermute | solution.py:86
  28.6 6.2 %collective-permute-start.11 = (bf16[64,512]{1,0:T(8,128)(2,1)S(1)}, bf16[64,512]{1,0:T(8,128)(2,1)S(1)}, u32[]{:S(2)}, u32[]{:S(2)}) collective-permute-start(bf16[64,512]{1,0:T(8,128)(2,1)S(1)} %fusion.1), channel_id=1, source_target_pairs={{0,24},{4,28},{8,16},{12,20},{16,8},{20,12},{24,0},{28,4},{1,25},{... | collective-permute-start | bytes 196616 | tf_op jit(solution)/shard_map/ppermute | solution.py:86
  30.0 4.8 %collective-permute-start.10 = (bf16[64,512]{1,0:T(8,128)(2,1)S(1)}, bf16[64,512]{1,0:T(8,128)(2,1)S(1)}, u32[]{:S(2)}, u32[]{:S(2)}) collective-permute-start(bf16[64,512]{1,0:T(8,128)(2,1)S(1)} %fusion.1), channel_id=1, source_target_pairs={{0,8},{4,12},{8,0},{12,4},{16,24},{20,28},{24,16},{28,20},{1,9},{5... | collective-permute-start | bytes 196616 | tf_op jit(solution)/shard_map/ppermute | solution.py:86
  34.8 1.4 %collective-permute-start.12 = (f32[64,512]{1,0:T(8,128)S(1)}, f32[64,512]{1,0:T(8,128)S(1)}, u32[]{:S(2)}, u32[]{:S(2)}) collective-permute-start(f32[64,512]{1,0:T(8,128)S(1)} %add_add_fusion), channel_id=1, source_target_pairs={{0,4},{4,0},{8,12},{12,8},{16,20},{20,16},{24,28},{28,24},{1,5},{5... | collective-permute-start | bytes 393224 | tf_op jit(solution)/shard_map/ppermute | solution.py:86

commit v5 on v4

--- a/solution.py
+++ b/solution.py
@@ -264,11 +264,12 @@
     along, even, odd = lax.optimization_barrier((along, even, odd))
     out = (pre * jax.nn.sigmoid(pre)).astype(BF16)
     total = (mine.astype(F32) + across) + (along + diagonal)
+    total = total.astype(BF16)
     rest = swap(total, "row", 1, 8)
     grad_features = (part + (odd.astype(F32) + even.astype(F32))).astype(BF16)
     first = jnp.where(half == 0, total, rest)
     second = jnp.where(half == 0, rest, total)
-    grad_weight = jnp.concatenate([first, second], axis=0)
+    grad_weight = jnp.concatenate([first, second], axis=0).astype(F32)
     return (out, grad_features, grad_weight)
 
 

time: 37.3 us -> 37.2 us (level)
    convert_element_type x0 -> x2, other arithmetic: none -> 0.77 us  [the longest x1 0.73 us: four_by_eight(): grad_weight = jnp.concatenate([first, second], axis=0).astype(F32)]
    concatenate x1 -> x0, other arithmetic: 0.72 us -> none  [four_by_eight(): grad_weight = jnp.concatenate([first, second], axis=0)]
where the time goes in v5:
time: 37.2 us; the launch traced here: 36.9 us
  starting transfers between devices  17.1 us (46%)
  waiting for transfers between devices  9.02 us (24%)
  Pallas kernels  3.61 us (10%)
  local copies, waits for them, and re-layouts  3.45 us (9%)
  other arithmetic  2.35 us (6%)
  between operations  1.42 us (4%)
    ppermute x11, starting transfers between devices, swap(): return lax.ppermute(value, axis, [(i, i ^ mask) for i in range(size)])  14.5 us
    ppermute x11, waiting for transfers between devices, swap(): return lax.ppermute(value, axis, [(i, i ^ mask) for i in range(size)])  5.57 us
    ppermute x1, waiting for transfers between devices, four_by_eight(): even = lax.ppermute(back, 'col', [(0, 2), (2, 0)])  3.44 us
    unnamed x10, local copies, waits for them, and re-layouts  3.44 us
    ppermute x1, starting transfers between devices, four_by_eight(): even = lax.ppermute(back, 'col', [(0, 2), (2, 0)])  1.93 us
    pallas_call x1, Pallas kernels, four_by_eight(): pl.pallas_call(functools.partial(pair_kernel, scale, slots), out_shape=(b...  1.24 us
    pallas_call x1, Pallas kernels, four_by_eight(): pl.pallas_call(backward_kernel, out_shape=(jax.ShapeDtypeStruct((rows, wi...  0.75 us
  transfers between devices with their start and end apart: 13, of which 7 were waited for; matrix products, arithmetic and copies ran while one was open for 4% of the time, Pallas kernels for 6%

profile of v5, /device:TPU:0, one launch (start us, length us, event | category | flops | bytes accessed | tf_op | source)
XLA Modules:
  0.0 36.9 jit_solution(1233531413500399819)
XLA Ops:
  0.6 3.1 %collective-permute-start = (bf16[128,512]{1,0:T(8,128)(2,1)}, bf16[128,512]{1,0:T(8,128)(2,1)S(1)}, u32[]{:S(2)}, u32[]{:S(2)}) collective-permute-start(bf16[128,512]{1,0:T(8,128)(2,1)} %f.1), channel_id=1, source_target_pairs={{0,1},{1,0},{2,3},{3,2},{4,5},{5,4},{6,7},{7,6},{8,9},{9,8},{10,11... | collective-permute-start | bytes 393224 | tf_op jit(solution)/shard_map/ppermute | solution.py:86
  3.7 2.6 %collective-permute-start.1 = (bf16[128,512]{1,0:T(8,128)(2,1)}, bf16[128,512]{1,0:T(8,128)(2,1)S(1)}, u32[]{:S(2)}, u32[]{:S(2)}) collective-permute-start(bf16[128,512]{1,0:T(8,128)(2,1)} %f.1), channel_id=1, source_target_pairs={{0,2},{1,3},{2,0},{3,1},{4,6},{5,7},{6,4},{7,5},{8,10},{9,11},{10,... | collective-permute-start | bytes 393224 | tf_op jit(solution)/shard_map/ppermute | solution.py:86
  6.3 0.9 %collective-permute-start.4 = (bf16[128,512]{1,0:T(8,128)(2,1)}, bf16[128,512]{1,0:T(8,128)(2,1)S(1)}, u32[]{:S(2)}, u32[]{:S(2)}) collective-permute-start(bf16[128,512]{1,0:T(8,128)(2,1)} %ct.1), channel_id=1, source_target_pairs={{0,1},{1,0},{2,3},{3,2},{4,5},{5,4},{6,7},{7,6},{8,9},{9,8},{10,11... | collective-permute-start | bytes 393224 | tf_op jit(solution)/shard_map/ppermute | solution.py:86
  7.9 0.8 %copy-done.3 = bf16[2,128,128]{2,1,0:T(8,128)(2,1)S(1)} copy-done((bf16[2,128,128]{2,1,0:T(8,128)(2,1)S(1)}, bf16[2,128,128]{2,1,0:T(8,128)(2,1)}, u32[]{:S(2)}) %copy-start.3) | copy-done | bytes 65560
  8.7 0.7 %copy-done.4 = s32[1,2]{1,0:T(1,128)S(1)} copy-done((s32[1,2]{1,0:T(1,128)S(1)}, s32[1,2]{1,0:T(1,128)}, u32[]{:S(2)}) %copy-start.4) | copy-done | bytes 32
  9.4 0.5 %shard_map.85.tp = bf16[288,128]{1,0:T(8,128)(2,1)S(1)} custom-call(s32[1,2]{1,0:T(1,128)S(1)} %copy-done.4, s32[1]{0:T(128)S(6)} %copy.9.count, bf16[2,128,128]{2,1,0:T(8,128)(2,1)S(1)} %copy-done.3), custom_call_target="tpu_custom_call" | custom-call | tf_op jit(solution)/shard_map/pallas_call | solution.py:187
  9.9 1.2 %collective-permute-start.3 = (bf16[288,128]{1,0:T(8,128)(2,1)S(1)}, bf16[288,128]{1,0:T(8,128)(2,1)S(1)}, u32[]{:S(2)}, u32[]{:S(2)}) collective-permute-start(bf16[288,128]{1,0:T(8,128)(2,1)S(1)} %shard_map.85.tp), channel_id=1, source_target_pairs={{0,1},{1,0},{2,3},{3,2},{4,5},{5,4},{6,7},{7,6},{8,9},{9,8},{10,11... | collective-permute-start | bytes 221192 | tf_op jit(solution)/shard_map/ppermute | solution.py:86
  11.2 1.0 %copy-done = bf16[512,512]{1,0:T(8,128)(2,1)S(1)} copy-done((bf16[512,512]{1,0:T(8,128)(2,1)S(1)}, bf16[512,512]{1,0:T(8,128)(2,1)}, u32[]{:S(2)}) %copy-start) | copy-done | bytes 524312
  12.2 0.9 %copy-done.2 = bf16[128,512]{1,0:T(8,128)(2,1)S(1)} copy-done((bf16[128,512]{1,0:T(8,128)(2,1)S(1)}, bf16[128,512]{1,0:T(8,128)(2,1)}, u32[]{:S(2)}) %copy-start.2) | copy-done | bytes 131096
  13.1 0.6 %shard_map.86 = (bf16[128,512]{1,0:T(8,128)(2,1)S(1)}, bf16[128,512]{1,0:T(8,128)(2,1)S(1)}, bf16[512,512]{1,0:T(8,128)(2,1)S(1)}, bf16[128,512]{1,0:T(8,128)(2,1)S(1)}) custom-call(s32[2]{0:T(128)S(1)} %pad_add_fusion.where, bf16[288,128]{1,0:T(8,128)(2,1)S(1)} %shard_map.85.tp, bf16[128,512]{1,0:T(8,128)(2,1)S(1)} %copy-done.1, ...), custom_call_target="tpu_custom_call" | custom-call | tf_op jit(solution)/shard_map/pallas_call | solution.py:195
  13.8 3.1 %collective-permute-done.1.f2 = bf16[128,512]{1,0:T(8,128)(2,1)S(1)} collective-permute-done((bf16[128,512]{1,0:T(8,128)(2,1)}, bf16[128,512]{1,0:T(8,128)(2,1)S(1)}, u32[]{:S(2)}, u32[]{:S(2)}) %collective-permute-start.1) | collective-permute-done | bytes 131104 | tf_op jit(solution)/shard_map/ppermute | solution.py:86
  17.4 1.2 %shard_map.88 = (bf16[128,512]{1,0:T(8,128)(2,1)S(1)}, bf16[128,512]{1,0:T(8,128)(2,1)S(1)}, f32[2,64,512]{2,1,0:T(8,128)S(1)}, bf16[2,64,512]{2,1,0:T(8,128)(2,1)S(1)}) custom-call(s32[2]{0:T(128)S(1)} %pad_add_fusion.where, bf16[256,512]{1,0:T(8,128)(2,1)S(1)} %get-tuple-element.30.near, bf16[256,512]{1,0:T(8,128)(2,1)S(1)} %get-tuple-element.31.far, ...), custom_call_target="tpu_custom_call" | custom-call | flops 268435456 | bytes 2097152 | tf_op jit(solution)/shard_map/pallas_call | solution.py:220
  18.8 1.3 %collective-permute-done.5 = bf16[2,64,512]{2,1,0:T(8,128)(2,1)S(1)} collective-permute-done((bf16[2,64,512]{2,1,0:T(8,128)(2,1)S(1)}, bf16[2,64,512]{2,1,0:T(8,128)(2,1)S(1)}, u32[]{:S(2)}, u32[]{:S(2)}) %collective-permute-start.5) | collective-permute-done | bytes 131104 | tf_op jit(solution)/shard_map/ppermute | solution.py:86
  20.2 3.0 %collective-permute-start.6 = (bf16[64,512]{1,0:T(8,128)(2,1)S(1)}, bf16[64,512]{1,0:T(8,128)(2,1)S(1)}, u32[]{:S(2)}, u32[]{:S(2)}) collective-permute-start(bf16[64,512]{1,0:T(8,128)(2,1)S(1)} %fusion.2), channel_id=1, source_target_pairs={{0,2},{1,3},{2,0},{3,1},{4,6},{5,7},{6,4},{7,5},{8,10},{9,11},{10,... | collective-permute-start | bytes 196616 | tf_op jit(solution)/shard_map/ppermute | solution.py:86
  23.2 0.7 %shard_map.89 = (bf16[128,512]{1,0:T(8,128)(2,1)S(1)}, f32[128,512]{1,0:T(8,128)S(1)}) custom-call(bf16[128,512]{1,0:T(8,128)(2,1)S(1)} %get-tuple-element.29.gp0, bf16[128,512]{1,0:T(8,128)(2,1)S(1)} %get-tuple-element.36.gp1, bf16[128,512]{1,0:T(8,128)(2,1)S(1)} %get-tuple-element.25.adj.adj0, bf16[128,512]{1,0:T(8,128)(2,1)S(1)} %get-tuple-element.37.adj1, ...), custom_call_target="tpu_custom_call" | custom-call | flops 268435456 | bytes 2097152 | tf_op jit(solution)/shard_map/pallas_call | solution.py:245
  23.9 1.9 %collective-permute-start.8 = (bf16[128,512]{1,0:T(8,128)(2,1)S(1)}, bf16[128,512]{1,0:T(8,128)(2,1)S(1)}, u32[]{:S(2)}, u32[]{:S(2)}) collective-permute-start(bf16[128,512]{1,0:T(8,128)(2,1)S(1)} %get-tuple-element.40), channel_id=1, source_target_pairs={{0,2},{2,0},{4,6},{6,4},{8,10},{10,8},{12,14},{14,12},{16,18},{18,... | collective-permute-start | bytes 393224 | tf_op jit(solution)/shard_map/ppermute | solution.py:259
  25.9 0.7 %collective-permute-start.9 = (bf16[128,512]{1,0:T(8,128)(2,1)S(1)}, bf16[128,512]{1,0:T(8,128)(2,1)S(1)}, u32[]{:S(2)}, u32[]{:S(2)}) collective-permute-start(bf16[128,512]{1,0:T(8,128)(2,1)S(1)} %get-tuple-element.40), channel_id=1, source_target_pairs={{1,3},{3,1},{5,7},{7,5},{9,11},{11,9},{13,15},{15,13},{17,19},{19,... | collective-permute-start | bytes 393224 | tf_op jit(solution)/shard_map/ppermute | solution.py:258
  27.0 1.6 %collective-permute-start.7 = (bf16[64,512]{1,0:T(8,128)(2,1)S(1)}, bf16[64,512]{1,0:T(8,128)(2,1)S(1)}, u32[]{:S(2)}, u32[]{:S(2)}) collective-permute-start(bf16[64,512]{1,0:T(8,128)(2,1)S(1)} %fusion.1), channel_id=1, source_target_pairs={{0,16},{4,20},{8,24},{12,28},{16,0},{20,4},{24,8},{28,12},{1,17},{... | collective-permute-start | bytes 196616 | tf_op jit(solution)/shard_map/ppermute | solution.py:86
  28.6 1.4 %collective-permute-start.11 = (bf16[64,512]{1,0:T(8,128)(2,1)S(1)}, bf16[64,512]{1,0:T(8,128)(2,1)S(1)}, u32[]{:S(2)}, u32[]{:S(2)}) collective-permute-start(bf16[64,512]{1,0:T(8,128)(2,1)S(1)} %fusion.1), channel_id=1, source_target_pairs={{0,24},{4,28},{8,16},{12,20},{16,8},{20,12},{24,0},{28,4},{1,25},{... | collective-permute-start | bytes 196616 | tf_op jit(solution)/shard_map/ppermute | solution.py:86
  30.0 0.5 %collective-permute-start.10 = (bf16[64,512]{1,0:T(8,128)(2,1)S(1)}, bf16[64,512]{1,0:T(8,128)(2,1)S(1)}, u32[]{:S(2)}, u32[]{:S(2)}) collective-permute-start(bf16[64,512]{1,0:T(8,128)(2,1)S(1)} %fusion.1), channel_id=1, source_target_pairs={{0,8},{4,12},{8,0},{12,4},{16,24},{20,28},{24,16},{28,20},{1,9},{5... | collective-permute-start | bytes 196616 | tf_op jit(solution)/shard_map/ppermute | solution.py:86
  30.5 0.7 %multiply_convert_fusion = bf16[128,512]{1,0:T(8,128)(2,1)} fusion(f32[128,512]{1,0:T(8,128)S(1)} %get-tuple-element.28), kind=kLoop, calls=%fused_computation.2 | loop fusion | flops 327680 | bytes 393216 | tf_op jit(solution)/shard_map/convert_element_type | solution.py:265
  31.3 3.4 %collective-permute-done.8 = bf16[128,512]{1,0:T(8,128)(2,1)S(1)} collective-permute-done((bf16[128,512]{1,0:T(8,128)(2,1)S(1)}, bf16[128,512]{1,0:T(8,128)(2,1)S(1)}, u32[]{:S(2)}, u32[]{:S(2)}) %collective-permute-start.8) | collective-permute-done | bytes 131104 | tf_op jit(solution)/shard_map/ppermute | solution.py:259
  34.9 0.7 %add_convert_fusion = bf16[128,512]{1,0:T(8,128)(2,1)} fusion(f32[128,512]{1,0:T(8,128)S(1)} %get-tuple-element.38, bf16[128,512]{1,0:T(8,128)(2,1)S(1)} %collective-permute-done.8, bf16[128,512]{1,0:T(8,128)(2,1)S(1)} %collective-permute-done.9), kind=kLoop, calls=%fused_computation | loop fusion | flops 327680 | bytes 655360 | tf_op jit(solution)/shard_map/convert_element_type | solution.py:269
  36.2 0.7 %maximum_convert_fusion = f32[128,512]{1,0:T(8,128)} fusion(bf16[64,512]{1,0:T(8,128)(2,1)S(1)} %get-tuple-element.46, bf16[64,512]{1,0:T(8,128)(2,1)S(1)} %get-tuple-element.45), kind=kLoop, calls=%fused_computation.7 | loop fusion | flops 262144 | bytes 393216 | tf_op jit(solution)/shard_map/convert_element_type | solution.py:272
  (27 shorter events, 1.9 us)
Async XLA Ops:
  0.6 10.6 %copy-start.1 = (bf16[128,512]{1,0:T(8,128)(2,1)S(1)}, bf16[128,512]{1,0:T(8,128)(2,1)}, u32[]{:S(2)}) copy-start(bf16[128,512]{1,0:T(8,128)(2,1)} %f.1) | copy-start | bytes 393220
  0.6 13.1 %collective-permute-start = (bf16[128,512]{1,0:T(8,128)(2,1)}, bf16[128,512]{1,0:T(8,128)(2,1)S(1)}, u32[]{:S(2)}, u32[]{:S(2)}) collective-permute-start(bf16[128,512]{1,0:T(8,128)(2,1)} %f.1), channel_id=1, source_target_pairs={{0,1},{1,0},{2,3},{3,2},{4,5},{5,4},{6,7},{7,6},{8,9},{9,8},{10,11... | collective-permute-start | bytes 393224 | tf_op jit(solution)/shard_map/ppermute | solution.py:86
  3.7 13.2 %collective-permute-start.1 = (bf16[128,512]{1,0:T(8,128)(2,1)}, bf16[128,512]{1,0:T(8,128)(2,1)S(1)}, u32[]{:S(2)}, u32[]{:S(2)}) collective-permute-start(bf16[128,512]{1,0:T(8,128)(2,1)} %f.1), channel_id=1, source_target_pairs={{0,2},{1,3},{2,0},{3,1},{4,6},{5,7},{6,4},{7,5},{8,10},{9,11},{10,... | collective-permute-start | bytes 393224 | tf_op jit(solution)/shard_map/ppermute | solution.py:86
  6.3 10.6 %collective-permute-start.2 = (bf16[128,512]{1,0:T(8,128)(2,1)}, bf16[128,512]{1,0:T(8,128)(2,1)S(1)}, u32[]{:S(2)}, u32[]{:S(2)}) collective-permute-start(bf16[128,512]{1,0:T(8,128)(2,1)} %f.1), channel_id=1, source_target_pairs={{0,3},{1,2},{2,1},{3,0},{4,7},{5,6},{6,5},{7,4},{8,11},{9,10},{10,... | collective-permute-start | bytes 393224 | tf_op jit(solution)/shard_map/ppermute | solution.py:86
  6.3 11.1 %collective-permute-start.4 = (bf16[128,512]{1,0:T(8,128)(2,1)}, bf16[128,512]{1,0:T(8,128)(2,1)S(1)}, u32[]{:S(2)}, u32[]{:S(2)}) collective-permute-start(bf16[128,512]{1,0:T(8,128)(2,1)} %ct.1), channel_id=1, source_target_pairs={{0,1},{1,0},{2,3},{3,2},{4,5},{5,4},{6,7},{7,6},{8,9},{9,8},{10,11... | collective-permute-start | bytes 393224 | tf_op jit(solution)/shard_map/ppermute | solution.py:86
  7.9 0.8 %copy-start.3 = (bf16[2,128,128]{2,1,0:T(8,128)(2,1)S(1)}, bf16[2,128,128]{2,1,0:T(8,128)(2,1)}, u32[]{:S(2)}) copy-start(bf16[2,128,128]{2,1,0:T(8,128)(2,1)} %blocks.1) | copy-start | bytes 196612
  8.7 0.7 %copy-start.4 = (s32[1,2]{1,0:T(1,128)S(1)}, s32[1,2]{1,0:T(1,128)}, u32[]{:S(2)}) copy-start(s32[1,2]{1,0:T(1,128)} %index.1) | copy-start | bytes 28
  9.9 7.5 %collective-permute-start.3 = (bf16[288,128]{1,0:T(8,128)(2,1)S(1)}, bf16[288,128]{1,0:T(8,128)(2,1)S(1)}, u32[]{:S(2)}, u32[]{:S(2)}) collective-permute-start(bf16[288,128]{1,0:T(8,128)(2,1)S(1)} %shard_map.85.tp), channel_id=1, source_target_pairs={{0,1},{1,0},{2,3},{3,2},{4,5},{5,4},{6,7},{7,6},{8,9},{9,8},{10,11... | collective-permute-start | bytes 221192 | tf_op jit(solution)/shard_map/ppermute | solution.py:86
  11.2 1.0 %copy-start = (bf16[512,512]{1,0:T(8,128)(2,1)S(1)}, bf16[512,512]{1,0:T(8,128)(2,1)}, u32[]{:S(2)}) copy-start(bf16[512,512]{1,0:T(8,128)(2,1)} %w.1) | copy-start | bytes 1572868
  12.2 0.9 %copy-start.2 = (bf16[128,512]{1,0:T(8,128)(2,1)S(1)}, bf16[128,512]{1,0:T(8,128)(2,1)}, u32[]{:S(2)}) copy-start(bf16[128,512]{1,0:T(8,128)(2,1)} %ct.1) | copy-start | bytes 393220
  18.7 1.4 %collective-permute-start.5 = (bf16[2,64,512]{2,1,0:T(8,128)(2,1)S(1)}, bf16[2,64,512]{2,1,0:T(8,128)(2,1)S(1)}, u32[]{:S(2)}, u32[]{:S(2)}) collective-permute-start(bf16[2,64,512]{2,1,0:T(8,128)(2,1)S(1)} %get-tuple-element.34), channel_id=1, source_target_pairs={{0,4},{4,0},{8,12},{12,8},{16,20},{20,16},{24,28},{28,24},{1,5},{5... | collective-permute-start | bytes 393224 | tf_op jit(solution)/shard_map/ppermute | solution.py:86
  20.2 6.8 %collective-permute-start.6 = (bf16[64,512]{1,0:T(8,128)(2,1)S(1)}, bf16[64,512]{1,0:T(8,128)(2,1)S(1)}, u32[]{:S(2)}, u32[]{:S(2)}) collective-permute-start(bf16[64,512]{1,0:T(8,128)(2,1)S(1)} %fusion.2), channel_id=1, source_target_pairs={{0,2},{1,3},{2,0},{3,1},{4,6},{5,7},{6,4},{7,5},{8,10},{9,11},{10,... | collective-permute-start | bytes 196616 | tf_op jit(solution)/shard_map/ppermute | solution.py:86
  23.9 10.9 %collective-permute-start.8 = (bf16[128,512]{1,0:T(8,128)(2,1)S(1)}, bf16[128,512]{1,0:T(8,128)(2,1)S(1)}, u32[]{:S(2)}, u32[]{:S(2)}) collective-permute-start(bf16[128,512]{1,0:T(8,128)(2,1)S(1)} %get-tuple-element.40), channel_id=1, source_target_pairs={{0,2},{2,0},{4,6},{6,4},{8,10},{10,8},{12,14},{14,12},{16,18},{18,... | collective-permute-start | bytes 393224 | tf_op jit(solution)/shard_map/ppermute | solution.py:259
  25.9 8.9 %collective-permute-start.9 = (bf16[128,512]{1,0:T(8,128)(2,1)S(1)}, bf16[128,512]{1,0:T(8,128)(2,1)S(1)}, u32[]{:S(2)}, u32[]{:S(2)}) collective-permute-start(bf16[128,512]{1,0:T(8,128)(2,1)S(1)} %get-tuple-element.40), channel_id=1, source_target_pairs={{1,3},{3,1},{5,7},{7,5},{9,11},{11,9},{13,15},{15,13},{17,19},{19,... | collective-permute-start | bytes 393224 | tf_op jit(solution)/shard_map/ppermute | solution.py:258
  27.0 4.3 %collective-permute-start.7 = (bf16[64,512]{1,0:T(8,128)(2,1)S(1)}, bf16[64,512]{1,0:T(8,128)(2,1)S(1)}, u32[]{:S(2)}, u32[]{:S(2)}) collective-permute-start(bf16[64,512]{1,0:T(8,128)(2,1)S(1)} %fusion.1), channel_id=1, source_target_pairs={{0,16},{4,20},{8,24},{12,28},{16,0},{20,4},{24,8},{28,12},{1,17},{... | collective-permute-start | bytes 196616 | tf_op jit(solution)/shard_map/ppermute | solution.py:86
  28.6 6.2 %collective-permute-start.11 = (bf16[64,512]{1,0:T(8,128)(2,1)S(1)}, bf16[64,512]{1,0:T(8,128)(2,1)S(1)}, u32[]{:S(2)}, u32[]{:S(2)}) collective-permute-start(bf16[64,512]{1,0:T(8,128)(2,1)S(1)} %fusion.1), channel_id=1, source_target_pairs={{0,24},{4,28},{8,16},{12,20},{16,8},{20,12},{24,0},{28,4},{1,25},{... | collective-permute-start | bytes 196616 | tf_op jit(solution)/shard_map/ppermute | solution.py:86
  30.0 4.8 %collective-permute-start.10 = (bf16[64,512]{1,0:T(8,128)(2,1)S(1)}, bf16[64,512]{1,0:T(8,128)(2,1)S(1)}, u32[]{:S(2)}, u32[]{:S(2)}) collective-permute-start(bf16[64,512]{1,0:T(8,128)(2,1)S(1)} %fusion.1), channel_id=1, source_target_pairs={{0,8},{4,12},{8,0},{12,4},{16,24},{20,28},{24,16},{28,20},{1,9},{5... | collective-permute-start | bytes 196616 | tf_op jit(solution)/shard_map/ppermute | solution.py:86
  34.8 1.3 %collective-permute-start.12 = (bf16[64,512]{1,0:T(8,128)(2,1)S(1)}, bf16[64,512]{1,0:T(8,128)(2,1)S(1)}, u32[]{:S(2)}, u32[]{:S(2)}) collective-permute-start(bf16[64,512]{1,0:T(8,128)(2,1)S(1)} %add_convert_fusion.1), channel_id=1, source_target_pairs={{0,4},{4,0},{8,12},{12,8},{16,20},{20,16},{24,28},{28,24},{1,5},{5... | collective-permute-start | bytes 196616 | tf_op jit(solution)/shard_map/ppermute | solution.py:86

commit v6 on v5

--- a/solution.py
+++ b/solution.py
@@ -261,7 +261,7 @@
     diagonal = swap(mine, "row", 6, 8).astype(F32)
     along = swap(mine, "row", 4, 8).astype(F32)
     across = swap(mine, "row", 2, 8).astype(F32)
-    along, even, odd = lax.optimization_barrier((along, even, odd))
+    across, even, odd = lax.optimization_barrier((across, even, odd))
     out = (pre * jax.nn.sigmoid(pre)).astype(BF16)
     total = (mine.astype(F32) + across) + (along + diagonal)
     total = total.astype(BF16)

time: 37.2 us -> 37.2 us (level)
  no operation moved by 1% of the time
where the time goes in v6:
time: 37.2 us; the launch traced here: 36.9 us
  starting transfers between devices  17.1 us (46%)
  waiting for transfers between devices  9.02 us (24%)
  Pallas kernels  3.61 us (10%)
  local copies, waits for them, and re-layouts  3.45 us (9%)
  other arithmetic  2.35 us (6%)
  between operations  1.42 us (4%)
    ppermute x11, starting transfers between devices, swap(): return lax.ppermute(value, axis, [(i, i ^ mask) for i in range(size)])  14.5 us
    ppermute x11, waiting for transfers between devices, swap(): return lax.ppermute(value, axis, [(i, i ^ mask) for i in range(size)])  5.68 us
    unnamed x10, local copies, waits for them, and re-layouts  3.44 us
    ppermute x1, waiting for transfers between devices, four_by_eight(): even = lax.ppermute(back, 'col', [(0, 2), (2, 0)])  3.34 us
    ppermute x1, starting transfers between devices, four_by_eight(): even = lax.ppermute(back, 'col', [(0, 2), (2, 0)])  1.93 us
    pallas_call x1, Pallas kernels, four_by_eight(): pl.pallas_call(functools.partial(pair_kernel, scale, slots), out_shape=(b...  1.24 us
    pallas_call x1, Pallas kernels, four_by_eight(): pl.pallas_call(backward_kernel, out_shape=(jax.ShapeDtypeStruct((rows, wi...  0.75 us
  transfers between devices with their start and end apart: 13, of which 7 were waited for; matrix products, arithmetic and copies ran while one was open for 4% of the time, Pallas kernels for 6%

profile of v6, /device:TPU:0, one launch (start us, length us, event | category | flops | bytes accessed | tf_op | source)
XLA Modules:
  0.0 36.9 jit_solution(8965830026351110931)
XLA Ops:
  0.6 3.1 %collective-permute-start = (bf16[128,512]{1,0:T(8,128)(2,1)}, bf16[128,512]{1,0:T(8,128)(2,1)S(1)}, u32[]{:S(2)}, u32[]{:S(2)}) collective-permute-start(bf16[128,512]{1,0:T(8,128)(2,1)} %f.1), channel_id=1, source_target_pairs={{0,1},{1,0},{2,3},{3,2},{4,5},{5,4},{6,7},{7,6},{8,9},{9,8},{10,11... | collective-permute-start | bytes 393224 | tf_op jit(solution)/shard_map/ppermute | solution.py:86
  3.7 2.6 %collective-permute-start.1 = (bf16[128,512]{1,0:T(8,128)(2,1)}, bf16[128,512]{1,0:T(8,128)(2,1)S(1)}, u32[]{:S(2)}, u32[]{:S(2)}) collective-permute-start(bf16[128,512]{1,0:T(8,128)(2,1)} %f.1), channel_id=1, source_target_pairs={{0,2},{1,3},{2,0},{3,1},{4,6},{5,7},{6,4},{7,5},{8,10},{9,11},{10,... | collective-permute-start | bytes 393224 | tf_op jit(solution)/shard_map/ppermute | solution.py:86
  6.3 0.9 %collective-permute-start.4 = (bf16[128,512]{1,0:T(8,128)(2,1)}, bf16[128,512]{1,0:T(8,128)(2,1)S(1)}, u32[]{:S(2)}, u32[]{:S(2)}) collective-permute-start(bf16[128,512]{1,0:T(8,128)(2,1)} %ct.1), channel_id=1, source_target_pairs={{0,1},{1,0},{2,3},{3,2},{4,5},{5,4},{6,7},{7,6},{8,9},{9,8},{10,11... | collective-permute-start | bytes 393224 | tf_op jit(solution)/shard_map/ppermute | solution.py:86
  7.9 0.8 %copy-done.3 = bf16[2,128,128]{2,1,0:T(8,128)(2,1)S(1)} copy-done((bf16[2,128,128]{2,1,0:T(8,128)(2,1)S(1)}, bf16[2,128,128]{2,1,0:T(8,128)(2,1)}, u32[]{:S(2)}) %copy-start.3) | copy-done | bytes 65560
  8.7 0.7 %copy-done.4 = s32[1,2]{1,0:T(1,128)S(1)} copy-done((s32[1,2]{1,0:T(1,128)S(1)}, s32[1,2]{1,0:T(1,128)}, u32[]{:S(2)}) %copy-start.4) | copy-done | bytes 32
  9.4 0.5 %shard_map.85.tp = bf16[288,128]{1,0:T(8,128)(2,1)S(1)} custom-call(s32[1,2]{1,0:T(1,128)S(1)} %copy-done.4, s32[1]{0:T(128)S(6)} %copy.9.count, bf16[2,128,128]{2,1,0:T(8,128)(2,1)S(1)} %copy-done.3), custom_call_target="tpu_custom_call" | custom-call | tf_op jit(solution)/shard_map/pallas_call | solution.py:187
  9.9 1.2 %collective-permute-start.3 = (bf16[288,128]{1,0:T(8,128)(2,1)S(1)}, bf16[288,128]{1,0:T(8,128)(2,1)S(1)}, u32[]{:S(2)}, u32[]{:S(2)}) collective-permute-start(bf16[288,128]{1,0:T(8,128)(2,1)S(1)} %shard_map.85.tp), channel_id=1, source_target_pairs={{0,1},{1,0},{2,3},{3,2},{4,5},{5,4},{6,7},{7,6},{8,9},{9,8},{10,11... | collective-permute-start | bytes 221192 | tf_op jit(solution)/shard_map/ppermute | solution.py:86
  11.2 1.0 %copy-done = bf16[512,512]{1,0:T(8,128)(2,1)S(1)} copy-done((bf16[512,512]{1,0:T(8,128)(2,1)S(1)}, bf16[512,512]{1,0:T(8,128)(2,1)}, u32[]{:S(2)}) %copy-start) | copy-done | bytes 524312
  12.2 0.9 %copy-done.2 = bf16[128,512]{1,0:T(8,128)(2,1)S(1)} copy-done((bf16[128,512]{1,0:T(8,128)(2,1)S(1)}, bf16[128,512]{1,0:T(8,128)(2,1)}, u32[]{:S(2)}) %copy-start.2) | copy-done | bytes 131096
  13.1 0.6 %shard_map.86 = (bf16[128,512]{1,0:T(8,128)(2,1)S(1)}, bf16[128,512]{1,0:T(8,128)(2,1)S(1)}, bf16[512,512]{1,0:T(8,128)(2,1)S(1)}, bf16[128,512]{1,0:T(8,128)(2,1)S(1)}) custom-call(s32[2]{0:T(128)S(1)} %pad_add_fusion.where, bf16[288,128]{1,0:T(8,128)(2,1)S(1)} %shard_map.85.tp, bf16[128,512]{1,0:T(8,128)(2,1)S(1)} %copy-done.1, ...), custom_call_target="tpu_custom_call" | custom-call | tf_op jit(solution)/shard_map/pallas_call | solution.py:195
  13.8 3.1 %collective-permute-done.1.f2 = bf16[128,512]{1,0:T(8,128)(2,1)S(1)} collective-permute-done((bf16[128,512]{1,0:T(8,128)(2,1)}, bf16[128,512]{1,0:T(8,128)(2,1)S(1)}, u32[]{:S(2)}, u32[]{:S(2)}) %collective-permute-start.1) | collective-permute-done | bytes 131104 | tf_op jit(solution)/shard_map/ppermute | solution.py:86
  17.4 1.2 %shard_map.88 = (bf16[128,512]{1,0:T(8,128)(2,1)S(1)}, bf16[128,512]{1,0:T(8,128)(2,1)S(1)}, f32[2,64,512]{2,1,0:T(8,128)S(1)}, bf16[2,64,512]{2,1,0:T(8,128)(2,1)S(1)}) custom-call(s32[2]{0:T(128)S(1)} %pad_add_fusion.where, bf16[256,512]{1,0:T(8,128)(2,1)S(1)} %get-tuple-element.30.near, bf16[256,512]{1,0:T(8,128)(2,1)S(1)} %get-tuple-element.31.far, ...), custom_call_target="tpu_custom_call" | custom-call | flops 268435456 | bytes 2097152 | tf_op jit(solution)/shard_map/pallas_call | solution.py:220
  18.8 1.3 %collective-permute-done.5 = bf16[2,64,512]{2,1,0:T(8,128)(2,1)S(1)} collective-permute-done((bf16[2,64,512]{2,1,0:T(8,128)(2,1)S(1)}, bf16[2,64,512]{2,1,0:T(8,128)(2,1)S(1)}, u32[]{:S(2)}, u32[]{:S(2)}) %collective-permute-start.5) | collective-permute-done | bytes 131104 | tf_op jit(solution)/shard_map/ppermute | solution.py:86
  20.2 3.0 %collective-permute-start.6 = (bf16[64,512]{1,0:T(8,128)(2,1)S(1)}, bf16[64,512]{1,0:T(8,128)(2,1)S(1)}, u32[]{:S(2)}, u32[]{:S(2)}) collective-permute-start(bf16[64,512]{1,0:T(8,128)(2,1)S(1)} %fusion.2), channel_id=1, source_target_pairs={{0,2},{1,3},{2,0},{3,1},{4,6},{5,7},{6,4},{7,5},{8,10},{9,11},{10,... | collective-permute-start | bytes 196616 | tf_op jit(solution)/shard_map/ppermute | solution.py:86
  23.2 0.7 %shard_map.89 = (bf16[128,512]{1,0:T(8,128)(2,1)S(1)}, f32[128,512]{1,0:T(8,128)S(1)}) custom-call(bf16[128,512]{1,0:T(8,128)(2,1)S(1)} %get-tuple-element.29.gp0, bf16[128,512]{1,0:T(8,128)(2,1)S(1)} %get-tuple-element.36.gp1, bf16[128,512]{1,0:T(8,128)(2,1)S(1)} %get-tuple-element.25.adj.adj0, bf16[128,512]{1,0:T(8,128)(2,1)S(1)} %get-tuple-element.37.adj1, ...), custom_call_target="tpu_custom_call" | custom-call | flops 268435456 | bytes 2097152 | tf_op jit(solution)/shard_map/pallas_call | solution.py:245
  23.9 1.9 %collective-permute-start.8 = (bf16[128,512]{1,0:T(8,128)(2,1)S(1)}, bf16[128,512]{1,0:T(8,128)(2,1)S(1)}, u32[]{:S(2)}, u32[]{:S(2)}) collective-permute-start(bf16[128,512]{1,0:T(8,128)(2,1)S(1)} %get-tuple-element.40), channel_id=1, source_target_pairs={{0,2},{2,0},{4,6},{6,4},{8,10},{10,8},{12,14},{14,12},{16,18},{18,... | collective-permute-start | bytes 393224 | tf_op jit(solution)/shard_map/ppermute | solution.py:259
  25.9 0.7 %collective-permute-start.9 = (bf16[128,512]{1,0:T(8,128)(2,1)S(1)}, bf16[128,512]{1,0:T(8,128)(2,1)S(1)}, u32[]{:S(2)}, u32[]{:S(2)}) collective-permute-start(bf16[128,512]{1,0:T(8,128)(2,1)S(1)} %get-tuple-element.40), channel_id=1, source_target_pairs={{1,3},{3,1},{5,7},{7,5},{9,11},{11,9},{13,15},{15,13},{17,19},{19,... | collective-permute-start | bytes 393224 | tf_op jit(solution)/shard_map/ppermute | solution.py:258
  27.0 1.6 %collective-permute-start.7 = (bf16[64,512]{1,0:T(8,128)(2,1)S(1)}, bf16[64,512]{1,0:T(8,128)(2,1)S(1)}, u32[]{:S(2)}, u32[]{:S(2)}) collective-permute-start(bf16[64,512]{1,0:T(8,128)(2,1)S(1)} %fusion.1), channel_id=1, source_target_pairs={{0,8},{4,12},{8,0},{12,4},{16,24},{20,28},{24,16},{28,20},{1,9},{5... | collective-permute-start | bytes 196616 | tf_op jit(solution)/shard_map/ppermute | solution.py:86
  28.5 1.5 %collective-permute-start.11 = (bf16[64,512]{1,0:T(8,128)(2,1)S(1)}, bf16[64,512]{1,0:T(8,128)(2,1)S(1)}, u32[]{:S(2)}, u32[]{:S(2)}) collective-permute-start(bf16[64,512]{1,0:T(8,128)(2,1)S(1)} %fusion.1), channel_id=1, source_target_pairs={{0,24},{4,28},{8,16},{12,20},{16,8},{20,12},{24,0},{28,4},{1,25},{... | collective-permute-start | bytes 196616 | tf_op jit(solution)/shard_map/ppermute | solution.py:86
  30.5 0.7 %multiply_convert_fusion = bf16[128,512]{1,0:T(8,128)(2,1)} fusion(f32[128,512]{1,0:T(8,128)S(1)} %get-tuple-element.28), kind=kLoop, calls=%fused_computation.2 | loop fusion | flops 327680 | bytes 393216 | tf_op jit(solution)/shard_map/convert_element_type | solution.py:265
  31.4 3.3 %collective-permute-done.8 = bf16[128,512]{1,0:T(8,128)(2,1)S(1)} collective-permute-done((bf16[128,512]{1,0:T(8,128)(2,1)S(1)}, bf16[128,512]{1,0:T(8,128)(2,1)S(1)}, u32[]{:S(2)}, u32[]{:S(2)}) %collective-permute-start.8) | collective-permute-done | bytes 131104 | tf_op jit(solution)/shard_map/ppermute | solution.py:259
  34.9 0.7 %add_convert_fusion = bf16[128,512]{1,0:T(8,128)(2,1)} fusion(f32[128,512]{1,0:T(8,128)S(1)} %get-tuple-element.38, bf16[128,512]{1,0:T(8,128)(2,1)S(1)} %collective-permute-done.8, bf16[128,512]{1,0:T(8,128)(2,1)S(1)} %collective-permute-done.9), kind=kLoop, calls=%fused_computation | loop fusion | flops 327680 | bytes 655360 | tf_op jit(solution)/shard_map/convert_element_type | solution.py:269
  35.6 0.5 %collective-permute-done.12 = bf16[64,512]{1,0:T(8,128)(2,1)S(1)} collective-permute-done((bf16[64,512]{1,0:T(8,128)(2,1)S(1)}, bf16[64,512]{1,0:T(8,128)(2,1)S(1)}, u32[]{:S(2)}, u32[]{:S(2)}) %collective-permute-start.12) | collective-permute-done | bytes 65568 | tf_op jit(solution)/shard_map/ppermute | solution.py:86
  36.2 0.7 %maximum_convert_fusion = f32[128,512]{1,0:T(8,128)} fusion(bf16[64,512]{1,0:T(8,128)(2,1)S(1)} %get-tuple-element.46, bf16[64,512]{1,0:T(8,128)(2,1)S(1)} %get-tuple-element.45), kind=kLoop, calls=%fused_computation.7 | loop fusion | flops 262144 | bytes 393216 | tf_op jit(solution)/shard_map/convert_element_type | solution.py:272
  (27 shorter events, 2.0 us)
Async XLA Ops:
  0.6 10.6 %copy-start.1 = (bf16[128,512]{1,0:T(8,128)(2,1)S(1)}, bf16[128,512]{1,0:T(8,128)(2,1)}, u32[]{:S(2)}) copy-start(bf16[128,512]{1,0:T(8,128)(2,1)} %f.1) | copy-start | bytes 393220
  0.6 13.1 %collective-permute-start = (bf16[128,512]{1,0:T(8,128)(2,1)}, bf16[128,512]{1,0:T(8,128)(2,1)S(1)}, u32[]{:S(2)}, u32[]{:S(2)}) collective-permute-start(bf16[128,512]{1,0:T(8,128)(2,1)} %f.1), channel_id=1, source_target_pairs={{0,1},{1,0},{2,3},{3,2},{4,5},{5,4},{6,7},{7,6},{8,9},{9,8},{10,11... | collective-permute-start | bytes 393224 | tf_op jit(solution)/shard_map/ppermute | solution.py:86
  3.7 13.2 %collective-permute-start.1 = (bf16[128,512]{1,0:T(8,128)(2,1)}, bf16[128,512]{1,0:T(8,128)(2,1)S(1)}, u32[]{:S(2)}, u32[]{:S(2)}) collective-permute-start(bf16[128,512]{1,0:T(8,128)(2,1)} %f.1), channel_id=1, source_target_pairs={{0,2},{1,3},{2,0},{3,1},{4,6},{5,7},{6,4},{7,5},{8,10},{9,11},{10,... | collective-permute-start | bytes 393224 | tf_op jit(solution)/shard_map/ppermute | solution.py:86
  6.3 10.6 %collective-permute-start.2 = (bf16[128,512]{1,0:T(8,128)(2,1)}, bf16[128,512]{1,0:T(8,128)(2,1)S(1)}, u32[]{:S(2)}, u32[]{:S(2)}) collective-permute-start(bf16[128,512]{1,0:T(8,128)(2,1)} %f.1), channel_id=1, source_target_pairs={{0,3},{1,2},{2,1},{3,0},{4,7},{5,6},{6,5},{7,4},{8,11},{9,10},{10,... | collective-permute-start | bytes 393224 | tf_op jit(solution)/shard_map/ppermute | solution.py:86
  6.3 11.1 %collective-permute-start.4 = (bf16[128,512]{1,0:T(8,128)(2,1)}, bf16[128,512]{1,0:T(8,128)(2,1)S(1)}, u32[]{:S(2)}, u32[]{:S(2)}) collective-permute-start(bf16[128,512]{1,0:T(8,128)(2,1)} %ct.1), channel_id=1, source_target_pairs={{0,1},{1,0},{2,3},{3,2},{4,5},{5,4},{6,7},{7,6},{8,9},{9,8},{10,11... | collective-permute-start | bytes 393224 | tf_op jit(solution)/shard_map/ppermute | solution.py:86
  7.9 0.8 %copy-start.3 = (bf16[2,128,128]{2,1,0:T(8,128)(2,1)S(1)}, bf16[2,128,128]{2,1,0:T(8,128)(2,1)}, u32[]{:S(2)}) copy-start(bf16[2,128,128]{2,1,0:T(8,128)(2,1)} %blocks.1) | copy-start | bytes 196612
  8.7 0.7 %copy-start.4 = (s32[1,2]{1,0:T(1,128)S(1)}, s32[1,2]{1,0:T(1,128)}, u32[]{:S(2)}) copy-start(s32[1,2]{1,0:T(1,128)} %index.1) | copy-start | bytes 28
  9.9 7.5 %collective-permute-start.3 = (bf16[288,128]{1,0:T(8,128)(2,1)S(1)}, bf16[288,128]{1,0:T(8,128)(2,1)S(1)}, u32[]{:S(2)}, u32[]{:S(2)}) collective-permute-start(bf16[288,128]{1,0:T(8,128)(2,1)S(1)} %shard_map.85.tp), channel_id=1, source_target_pairs={{0,1},{1,0},{2,3},{3,2},{4,5},{5,4},{6,7},{7,6},{8,9},{9,8},{10,11... | collective-permute-start | bytes 221192 | tf_op jit(solution)/shard_map/ppermute | solution.py:86
  11.2 1.0 %copy-start = (bf16[512,512]{1,0:T(8,128)(2,1)S(1)}, bf16[512,512]{1,0:T(8,128)(2,1)}, u32[]{:S(2)}) copy-start(bf16[512,512]{1,0:T(8,128)(2,1)} %w.1) | copy-start | bytes 1572868
  12.2 0.9 %copy-start.2 = (bf16[128,512]{1,0:T(8,128)(2,1)S(1)}, bf16[128,512]{1,0:T(8,128)(2,1)}, u32[]{:S(2)}) copy-start(bf16[128,512]{1,0:T(8,128)(2,1)} %ct.1) | copy-start | bytes 393220
  18.7 1.4 %collective-permute-start.5 = (bf16[2,64,512]{2,1,0:T(8,128)(2,1)S(1)}, bf16[2,64,512]{2,1,0:T(8,128)(2,1)S(1)}, u32[]{:S(2)}, u32[]{:S(2)}) collective-permute-start(bf16[2,64,512]{2,1,0:T(8,128)(2,1)S(1)} %get-tuple-element.34), channel_id=1, source_target_pairs={{0,4},{4,0},{8,12},{12,8},{16,20},{20,16},{24,28},{28,24},{1,5},{5... | collective-permute-start | bytes 393224 | tf_op jit(solution)/shard_map/ppermute | solution.py:86
  20.2 6.8 %collective-permute-start.6 = (bf16[64,512]{1,0:T(8,128)(2,1)S(1)}, bf16[64,512]{1,0:T(8,128)(2,1)S(1)}, u32[]{:S(2)}, u32[]{:S(2)}) collective-permute-start(bf16[64,512]{1,0:T(8,128)(2,1)S(1)} %fusion.2), channel_id=1, source_target_pairs={{0,2},{1,3},{2,0},{3,1},{4,6},{5,7},{6,4},{7,5},{8,10},{9,11},{10,... | collective-permute-start | bytes 196616 | tf_op jit(solution)/shard_map/ppermute | solution.py:86
  23.9 10.9 %collective-permute-start.8 = (bf16[128,512]{1,0:T(8,128)(2,1)S(1)}, bf16[128,512]{1,0:T(8,128)(2,1)S(1)}, u32[]{:S(2)}, u32[]{:S(2)}) collective-permute-start(bf16[128,512]{1,0:T(8,128)(2,1)S(1)} %get-tuple-element.40), channel_id=1, source_target_pairs={{0,2},{2,0},{4,6},{6,4},{8,10},{10,8},{12,14},{14,12},{16,18},{18,... | collective-permute-start | bytes 393224 | tf_op jit(solution)/shard_map/ppermute | solution.py:259
  25.9 8.9 %collective-permute-start.9 = (bf16[128,512]{1,0:T(8,128)(2,1)S(1)}, bf16[128,512]{1,0:T(8,128)(2,1)S(1)}, u32[]{:S(2)}, u32[]{:S(2)}) collective-permute-start(bf16[128,512]{1,0:T(8,128)(2,1)S(1)} %get-tuple-element.40), channel_id=1, source_target_pairs={{1,3},{3,1},{5,7},{7,5},{9,11},{11,9},{13,15},{15,13},{17,19},{19,... | collective-permute-start | bytes 393224 | tf_op jit(solution)/shard_map/ppermute | solution.py:258
  27.0 4.4 %collective-permute-start.7 = (bf16[64,512]{1,0:T(8,128)(2,1)S(1)}, bf16[64,512]{1,0:T(8,128)(2,1)S(1)}, u32[]{:S(2)}, u32[]{:S(2)}) collective-permute-start(bf16[64,512]{1,0:T(8,128)(2,1)S(1)} %fusion.1), channel_id=1, source_target_pairs={{0,8},{4,12},{8,0},{12,4},{16,24},{20,28},{24,16},{28,20},{1,9},{5... | collective-permute-start | bytes 196616 | tf_op jit(solution)/shard_map/ppermute | solution.py:86
  28.5 6.3 %collective-permute-start.11 = (bf16[64,512]{1,0:T(8,128)(2,1)S(1)}, bf16[64,512]{1,0:T(8,128)(2,1)S(1)}, u32[]{:S(2)}, u32[]{:S(2)}) collective-permute-start(bf16[64,512]{1,0:T(8,128)(2,1)S(1)} %fusion.1), channel_id=1, source_target_pairs={{0,24},{4,28},{8,16},{12,20},{16,8},{20,12},{24,0},{28,4},{1,25},{... | collective-permute-start | bytes 196616 | tf_op jit(solution)/shard_map/ppermute | solution.py:86
  30.0 4.8 %collective-permute-start.10 = (bf16[64,512]{1,0:T(8,128)(2,1)S(1)}, bf16[64,512]{1,0:T(8,128)(2,1)S(1)}, u32[]{:S(2)}, u32[]{:S(2)}) collective-permute-start(bf16[64,512]{1,0:T(8,128)(2,1)S(1)} %fusion.1), channel_id=1, source_target_pairs={{0,16},{4,20},{8,24},{12,28},{16,0},{20,4},{24,8},{28,12},{1,17},{... | collective-permute-start | bytes 196616 | tf_op jit(solution)/shard_map/ppermute | solution.py:86
  34.8 1.3 %collective-permute-start.12 = (bf16[64,512]{1,0:T(8,128)(2,1)S(1)}, bf16[64,512]{1,0:T(8,128)(2,1)S(1)}, u32[]{:S(2)}, u32[]{:S(2)}) collective-permute-start(bf16[64,512]{1,0:T(8,128)(2,1)S(1)} %add_convert_fusion.1), channel_id=1, source_target_pairs={{0,4},{4,0},{8,12},{12,8},{16,20},{20,16},{24,28},{28,24},{1,5},{5... | collective-permute-start | bytes 196616 | tf_op jit(solution)/shard_map/ppermute | solution.py:86
